TPU v7x, 32 devices: a whole 2x2x4 slice. The times are simulated.
32 devices in a mesh: groups: 2 (over x), tile: 8 (over z, y), rot: 2 (over core).
Axes of the slice: x: 2, y: 2, z: 4, core: 2. Of those that a mesh axis runs over, the one named last changes fastest.
Arguments:
- features: bfloat16 [256, 512, 8, 64], P(('groups', 'tile'), None, 'rot'), parts along dimension 0, may hold values from -6 to 6
- weight: bfloat16 [8, 9, 64, 64], replicated, may hold values from -0.09375 to 0.09375
- bias: float32 [64], replicated, may hold values from -1 to 1
Outputs:
- output: bfloat16 [256, 512, 8, 64], P(('groups', 'tile'), None, 'rot'), parts along dimension 0
There are 2 independent parts, one for each index of `groups`. A program takes and returns all parts, laid end to end along the dimension named above; an argument that names none is the same for every part. Nothing has to cross between parts.
All inputs are finite; a program needn't handle non-finite values.
Results may differ from a plain program's by a relative error of at most 0.001.
Values may be sent and summed in bfloat16 or wider, within the bound.
No kernel may reach another device: no remote copies, remote signals or barrier semaphores. Data moves between devices by JAX's collectives and lax.ppermute only.
A program may use at most 256 MiB of HBM per device.

v0:
```python
import jax
import jax.numpy as jnp
import numpy as np
from jax import lax
from jax.sharding import PartitionSpec as P


def with_halo(cells, sides, width):
    for axis, dim in sides:
        count = lax.axis_size(axis)
        ends = count - 1
        head = lax.slice_in_dim(cells, 0, width, axis=dim)
        tail = lax.slice_in_dim(cells, cells.shape[dim] - width, cells.shape[dim], axis=dim)
        cells = jnp.concatenate(
            [
                lax.ppermute(tail, axis, [(i, (i + 1) % count) for i in range(ends)]),
                cells,
                lax.ppermute(head, axis, [((i + 1) % count, i) for i in range(ends)]),
            ],
            axis=dim,
        )
    return cells


def source_table():
    cycle = [5, 2, 1, 0, 3, 6, 7, 8]
    table = np.zeros((8, 9), np.int32)
    for turn in range(8):
        table[turn, 4] = 4
        for place in range(8):
            table[turn, cycle[place]] = cycle[(place - turn) % 8]
    return table


def build_filters(weight, inputs, outputs):
    table = jnp.asarray(source_table())
    relative = (inputs[:, None] - outputs[None, :]) % 8
    taps = table[outputs % 8]
    picked = weight[relative[:, None, :], jnp.transpose(taps)[None, :, :]]
    picked = jnp.transpose(picked, (0, 1, 3, 2, 4))
    count, ntaps, chans, nout, width = picked.shape
    return picked.reshape(count, ntaps, chans, nout * width)


def convolve(padded, filters):
    padded = jnp.pad(padded, ((0, 0), (1, 1), (0, 0), (0, 0)))
    rows = padded.shape[0] - 2
    cols = padded.shape[1] - 2
    count = padded.shape[2]
    chans = padded.shape[3]
    total = jnp.zeros((rows * cols, filters.shape[3]), jnp.float32)
    for row_off in range(3):
        for col_off in range(3):
            tap = row_off * 3 + col_off
            window = padded[row_off : row_off + rows, col_off : col_off + cols].reshape(
                rows * cols, count * chans
            )
            total = total + jnp.dot(
                window,
                filters[:, tap].reshape(count * chans, filters.shape[3]),
                preferred_element_type=jnp.float32,
            )
    return total


def local(features, weight, bias):
    rows, cols, owned, chans = features.shape
    here = lax.axis_index("rot")
    mine = here * owned + jnp.arange(owned, dtype=jnp.int32)
    padded = with_halo(features, (("tile", 0),), 1)
    filters = build_filters(weight, mine, jnp.arange(8, dtype=jnp.int32))
    terms = convolve(padded, filters).reshape(rows, cols, 8, chans)
    total = lax.psum_scatter(terms, "rot", scatter_dimension=2, tiled=True)
    return jnp.maximum(total + bias, 0.0).astype(jnp.bfloat16)


def solution(mesh):
    return jax.shard_map(
        local,
        mesh=mesh,
        in_specs=(P(("groups", "tile"), None, "rot", None), P(), P()),
        out_specs=P(("groups", "tile"), None, "rot", None),
        check_vma=False,
    )
```

profile of v0, /device:TPU:19, one launch (start us, length us, event | category | flops | bytes accessed | tf_op | source)
XLA Modules:
  0.0 349.6 jit_solution(8060937758324552269)
XLA Ops:
  6.5 0.0 copy-start
  6.5 0.0 reduce-scatter.2.cloned.1.call-start
  6.5 2.0 fusion.17
  8.5 3.1 collective-permute-start
  11.6 3.0 collective-permute-start.1
  14.7 0.0 copy-start.17
  14.7 6.6 %copy.14 = bf16[16,512,4,64]{1,0,3,2:T(8,128)(2,1)} copy(bf16[16,512,4,64]{1,3,2,0:T(8,128)(2,1)} %param.4) | data formatting | bytes 8388608 | tf_op args[0]
  21.3 0.0 copy-done.17
  21.3 0.6 gather_fusion
  21.9 0.1 copy.9
  22.0 0.1 fusion.14
  22.1 0.1 reshape.114
  22.2 0.0 copy-done
  22.2 6.4 %gather_fusion.1 = bf16[288,64,64]{2,1,0:T(8,128)(2,1)} fusion(bf16[8,9,64,64]{3,2,1,0:T(8,128)(2,1)S(1)} %copy-done, s32[288]{0:T(512)S(1)} %reshape.114), kind=kCustom, calls=%fused_computation.1 | custom fusion | bytes 4720896 | tf_op jit(solution)/shard_map/gather | solution.py:39
  28.6 13.8 %copy.34 = bf16[4,9,8,64,64]{4,2,3,1,0:T(8,128)(2,1)} copy(bf16[4,9,8,64,64]{4,3,2,1,0:T(8,128)(2,1)} %bitcast.101) | data formatting | bytes 4718592 | tf_op jit(solution)/shard_map/gather | solution.py:39
  42.4 6.4 %reshape.96 = bf16[4,9,64,512]{3,2,1,0:T(8,128)(2,1)S(1)} reshape(bf16[4,9,64,8,64]{4,3,2,1,0:T(8,128)(2,1)} %bitcast.102) | data formatting | bytes 4718592 | tf_op jit(solution)/shard_map/reshape | solution.py:42
  48.8 8.4 %copy.27 = bf16[32,8,16,512]{3,1,2,0:T(8,128)(2,1)} copy(bf16[32,8,16,512]{3,2,1,0:T(8,128)(2,1)} %bitcast.104) | data formatting | bytes 8388608
  57.2 1.1 fusion.18
  58.3 0.0 collective-permute-done
  58.3 0.0 collective-permute-done.1
  58.3 1.5 copy-done.2
  59.9 8.1 %fusion.9 = bf16[18,514,4,64]{1,3,2,0:T(8,128)(2,1)} fusion(bf16[1,512,4,64]{1,3,2,0:T(8,128)(2,1)} %collective-permute-done.1, bf16[16,512,4,64]{1,3,2,0:T(8,128)(2,1)S(1)} %copy-done.2, bf16[1,512,4,64]{1,3,2,0:T(8,128)(2,1)} %collective-permute-done), kind=kLoop, calls=%fused_computation.15 | loop fusion | flops 28422144 | bytes 9455616 | tf_op jit(solution)/shard_map/concatenate | solution.py:14
  68.0 19.5 %fusion.16 = (bf16[16,512,4,64]{1,3,2,0:T(8,128)(2,1)}, bf16[16,512,4,64]{1,3,2,0:T(8,128)(2,1)}, bf16[16,512,4,64]{1,3,2,0:T(8,128)(2,1)}, bf16[16,512,4,64]{1,...) fusion(bf16[18,514,4,64]{1,3,2,0:T(8,128)(2,1)} %fusion.9), kind=kLoop, calls=%fused_computation.35 | loop fusion | bytes 50331648 | tf_op jit(solution)/shard_map/slice | solution.py:55
  87.5 4.6 %copy.8 = bf16[16,512,4,64]{1,0,3,2:T(8,128)(2,1)S(1)} copy(bf16[16,512,4,64]{1,3,2,0:T(8,128)(2,1)} %get-tuple-element.5) | data formatting | bytes 8388608 | tf_op jit(solution)/shard_map/slice | solution.py:55
  92.1 0.0 copy-start.8
  92.1 4.4 %copy.23 = bf16[32,8,16,512]{3,1,2,0:T(8,128)(2,1)S(1)} copy(bf16[32,8,16,512]{3,2,1,0:T(8,128)(2,1)S(1)} %bitcast.105) | data formatting | bytes 8388608
  96.4 0.0 copy-done.8
  96.5 2.4 copy.12
  98.9 4.5 %copy.25 = bf16[32,8,16,512]{3,1,2,0:T(8,128)(2,1)S(1)} copy(bf16[32,8,16,512]{3,2,1,0:T(8,128)(2,1)S(1)} %bitcast.106) | data formatting | bytes 8388608
  103.5 2.4 copy.13
  105.9 4.4 %copy.26 = bf16[32,8,16,512]{3,1,2,0:T(8,128)(2,1)S(1)} copy(bf16[32,8,16,512]{3,2,1,0:T(8,128)(2,1)S(1)} %bitcast.107) | data formatting | bytes 8388608
  110.3 2.4 copy.16
  112.7 4.7 %copy.28 = bf16[32,8,16,512]{3,1,2,0:T(8,128)(2,1)S(1)} copy(bf16[32,8,16,512]{3,2,1,0:T(8,128)(2,1)S(1)} %bitcast.108) | data formatting | bytes 8388608
  117.5 2.4 copy.17
  119.9 6.4 %copy.29 = bf16[32,8,16,512]{3,1,2,0:T(8,128)(2,1)} copy(bf16[32,8,16,512]{3,2,1,0:T(8,128)(2,1)S(1)} %bitcast.109) | data formatting | bytes 8388608
  126.3 0.0 copy-done.4
  126.3 2.6 copy.19
  128.9 0.0 copy-start.3
  129.0 6.4 %copy.31 = bf16[32,8,16,512]{3,1,2,0:T(8,128)(2,1)} copy(bf16[32,8,16,512]{3,2,1,0:T(8,128)(2,1)S(1)} %bitcast.110) | data formatting | bytes 8388608
  135.3 1.7 pad_maximum_fusion.1
  137.1 2.4 copy.11
  139.5 4.3 %copy.24 = bf16[32,8,16,512]{3,1,2,0:T(8,128)(2,1)S(1)} copy(bf16[32,8,16,512]{3,2,1,0:T(8,128)(2,1)S(1)} %bitcast.111) | data formatting | bytes 8388608
  143.8 2.4 copy.18
  146.2 6.7 %copy.30 = bf16[32,8,16,512]{3,1,2,0:T(8,128)(2,1)} copy(bf16[32,8,16,512]{3,2,1,0:T(8,128)(2,1)S(1)} %bitcast.112) | data formatting | bytes 8388608
  152.9 8.1 %fusion.19 = f32[8192,512]{1,0:T(8,128)} fusion(bf16[8192,256]{0,1:T(8,128)(2,1)S(1)} %bitcast.113, bf16[256,512]{1,0:T(8,128)(2,1)S(1)} %bitcast.129), kind=kOutput, calls=%fused_computation.38 | convolution fusion | flops 2147483648 | bytes 21233664 | tf_op jit(solution)/shard_map/dot_general | solution.py:58
  161.1 0.0 copy-done.15
  161.1 8.1 %fusion.21 = f32[8192,512]{1,0:T(8,128)} fusion(bf16[8192,256]{0,1:T(8,128)(2,1)S(1)} %bitcast.114, bf16[256,512]{1,0:T(8,128)(2,1)S(1)} %bitcast.128), kind=kOutput, calls=%fused_computation.40 | convolution fusion | flops 2147483648 | bytes 21233664 | tf_op jit(solution)/shard_map/dot_general | solution.py:58
  169.2 8.1 %fusion.22 = f32[8192,512]{1,0:T(8,128)} fusion(bf16[8192,256]{0,1:T(8,128)(2,1)S(1)} %bitcast.115, bf16[256,512]{1,0:T(8,128)(2,1)S(1)} %bitcast.127), kind=kOutput, calls=%fused_computation.41 | convolution fusion | flops 2147483648 | bytes 21233664 | tf_op jit(solution)/shard_map/dot_general | solution.py:58
  177.3 0.0 copy-done.13
  177.3 8.1 %fusion.23 = f32[8192,512]{1,0:T(8,128)} fusion(bf16[8192,256]{0,1:T(8,128)(2,1)S(1)} %bitcast.116, bf16[256,512]{1,0:T(8,128)(2,1)S(1)} %bitcast.126), kind=kOutput, calls=%fused_computation.42 | convolution fusion | flops 2147483648 | bytes 21233664 | tf_op jit(solution)/shard_map/dot_general | solution.py:58
  185.4 0.0 copy-done.12
  185.4 8.4 %fusion.24 = f32[8192,512]{1,0:T(8,128)} fusion(bf16[8192,256]{0,1:T(8,128)(2,1)S(1)} %bitcast.117, bf16[256,512]{1,0:T(8,128)(2,1)S(1)} %bitcast.125), kind=kOutput, calls=%fused_computation.43 | convolution fusion | flops 2147483648 | bytes 21233664 | tf_op jit(solution)/shard_map/dot_general | solution.py:58
  193.8 0.0 copy-done.10
  193.8 8.1 %fusion.26 = f32[8192,512]{1,0:T(8,128)} fusion(bf16[8192,256]{0,1:T(8,128)(2,1)S(1)} %bitcast.118, bf16[256,512]{1,0:T(8,128)(2,1)S(1)} %bitcast.124), kind=kOutput, calls=%fused_computation.45 | convolution fusion | flops 2147483648 | bytes 21233664 | tf_op jit(solution)/shard_map/dot_general | solution.py:58
  201.9 8.2 %fusion.20 = f32[8192,512]{1,0:T(8,128)} fusion(bf16[8192,256]{0,1:T(8,128)(2,1)S(1)} %bitcast.119, bf16[256,512]{1,0:T(8,128)(2,1)S(1)} %bitcast.123), kind=kOutput, calls=%fused_computation.39 | convolution fusion | flops 2147483648 | bytes 21233664 | tf_op jit(solution)/shard_map/dot_general | solution.py:58
  210.1 8.1 %fusion.25 = f32[8192,512]{1,0:T(8,128)} fusion(bf16[8192,256]{0,1:T(8,128)(2,1)S(1)} %bitcast.120, bf16[256,512]{1,0:T(8,128)(2,1)S(1)} %bitcast.122), kind=kOutput, calls=%fused_computation.44 | convolution fusion | flops 2147483648 | bytes 21233664 | tf_op jit(solution)/shard_map/dot_general | solution.py:58
  218.3 49.7 %fusion.3 = f32[8192,512]{1,0:T(8,128)} fusion(f32[8192,512]{1,0:T(8,128)} %fusion.26, f32[8192,512]{1,0:T(8,128)} %fusion.25, f32[8192,512]{1,0:T(8,128)} %fusion.24, f32[8192,512]{1,0:T(8,128)} %fusion.23, f32[8192,512]{1,0:T(8,128)} %fusion.22, f32[8192,512]{1,0:T(8,128)} %fusion.21, f32[8192,512]{1,0:T(8,128)} %fusion.19, f32[8192,512]{1,0:T(8,128)} %fusion.20, ...), kind=kOutput, calls=%fused_computation.8 | convolution fusion | flops 2181038080 | bytes 155451392 | tf_op jit(solution)/shard_map/dot_general | solution.py:58
  267.9 17.4 %copy.20 = f32[8192,512]{0,1:T(8,128)} copy(f32[8192,512]{1,0:T(8,128)} %fusion.3) | data formatting | bytes 33554432 | tf_op jit(solution)/shard_map/add | solution.py:58
  285.4 20.2 %copy.32 = f32[64,8,16,512]{3,2,1,0:T(8,128)} copy(f32[64,8,16,512]{3,1,2,0:T(8,128)} %bitcast.100) | data formatting | bytes 33554432
  305.6 0.0 reduce-scatter.2.cloned.1.call-update
  305.6 27.3 %reduce-scatter.2.cloned.1.call-done = f32[16,512,4,64]{1,0,3,2:T(8,128)} async-done(((f32[16,512,8,64]{1,0,3,2:T(8,128)}), f32[16,512,4,64]{1,0,3,2:T(8,128)}) %reduce-scatter.2.cloned.1.call-update) | async-done | bytes 8388624 | tf_op jit(solution)/shard_map/reduce_scatter | solution.py:73
  332.9 0.0 copy-done.18
  332.9 5.2 %maximum_convert_fusion = bf16[16,512,4,64]{1,0,3,2:T(8,128)(2,1)S(1)} fusion(f32[16,512,4,64]{1,0,3,2:T(8,128)} %reduce-scatter.2.cloned.1.call-done, f32[64]{0:T(128)S(1)} %copy-done.18), kind=kLoop, calls=%fused_computation.10 | loop fusion | flops 6291456 | bytes 12583168 | tf_op jit(solution)/shard_map/convert_element_type | solution.py:74
  338.2 4.4 %copy.21 = bf16[16,512,4,64]{1,3,2,0:T(8,128)(2,1)} copy(bf16[16,512,4,64]{1,0,3,2:T(8,128)(2,1)S(1)} %maximum_convert_fusion) | data formatting | bytes 8388608 | tf_op jit(solution)/shard_map/convert_element_type | solution.py:74
  (29 shorter events, 0.1 us)
Async XLA Ops:
  6.5 15.6 %copy-start = (bf16[8,9,64,64]{3,2,1,0:T(8,128)(2,1)S(1)}, bf16[8,9,64,64]{3,2,1,0:T(8,128)(2,1)}, u32[]{:S(2)}) copy-start(bf16[8,9,64,64]{3,2,1,0:T(8,128)(2,1)} %param.5) | copy-start | bytes 1769476
  6.5 326.4 %reduce-scatter.2.cloned.1.call-start = ((), (), s32[]{:S(2)}) async-start(), calls=%async_computation.1 | async-start | bytes 25165824 | tf_op jit(solution)/shard_map/reduce_scatter | solution.py:73
  8.5 49.8 %collective-permute-start = (bf16[1,512,4,64]{1,3,2,0:T(8,128)(2,1)}, bf16[1,512,4,64]{1,3,2,0:T(8,128)(2,1)}, u32[]{:S(2)}, u32[]{:S(2)}) collective-permute-start(bf16[1,512,4,64]{1,3,2,0:T(8,128)(2,1)} %get-tuple-element.13), channel_id=1, source_target_pairs={{0,2},{2,4},{4,6},{6,8},{8,10},{10,12},{12,14},{1,3},{3,5},{5,7},{... | collective-permute-start | bytes 786440 | tf_op jit(solution)/shard_map/ppermute | solution.py:16
  11.6 46.7 %collective-permute-start.1 = (bf16[1,512,4,64]{1,3,2,0:T(8,128)(2,1)}, bf16[1,512,4,64]{1,3,2,0:T(8,128)(2,1)}, u32[]{:S(2)}, u32[]{:S(2)}) collective-permute-start(bf16[1,512,4,64]{1,3,2,0:T(8,128)(2,1)} %get-tuple-element.14), channel_id=1, source_target_pairs={{2,0},{4,2},{6,4},{8,6},{10,8},{12,10},{14,12},{3,1},{5,3},{7,5},{... | collective-permute-start | bytes 786440 | tf_op jit(solution)/shard_map/ppermute | solution.py:18
  14.7 6.6 %copy-start.17 = (s32[8,9]{1,0:T(8,128)S(1)}, s32[8,9]{1,0:T(8,128)}, u32[]{:S(2)}) copy-start(s32[8,9]{1,0:T(8,128)} %constant.44.clone) | copy-start | bytes 868
  57.2 2.7 copy-start.2
  92.1 4.4 %copy-start.8 = (bf16[16,512,4,64]{1,3,2,0:T(8,128)(2,1)S(1)}, bf16[16,512,4,64]{1,3,2,0:T(8,128)(2,1)}, u32[]{:S(2)}) copy-start(bf16[16,512,4,64]{1,3,2,0:T(8,128)(2,1)} %get-tuple-element.9) | copy-start | bytes 12582916
  98.9 4.6 %copy-start.7 = (bf16[16,512,4,64]{1,3,2,0:T(8,128)(2,1)S(1)}, bf16[16,512,4,64]{1,3,2,0:T(8,128)(2,1)}, u32[]{:S(2)}) copy-start(bf16[16,512,4,64]{1,3,2,0:T(8,128)(2,1)} %get-tuple-element.8) | copy-start | bytes 12582916
  105.9 4.4 %copy-start.6 = (bf16[16,512,4,64]{1,3,2,0:T(8,128)(2,1)S(1)}, bf16[16,512,4,64]{1,3,2,0:T(8,128)(2,1)}, u32[]{:S(2)}) copy-start(bf16[16,512,4,64]{1,3,2,0:T(8,128)(2,1)} %get-tuple-element.7) | copy-start | bytes 12582916
  112.7 4.8 %copy-start.5 = (bf16[16,512,4,64]{1,3,2,0:T(8,128)(2,1)S(1)}, bf16[16,512,4,64]{1,3,2,0:T(8,128)(2,1)}, u32[]{:S(2)}) copy-start(bf16[16,512,4,64]{1,3,2,0:T(8,128)(2,1)} %get-tuple-element.6) | copy-start | bytes 12582916
  119.9 6.4 %copy-start.4 = (bf16[16,512,4,64]{1,3,2,0:T(8,128)(2,1)S(1)}, bf16[16,512,4,64]{1,3,2,0:T(8,128)(2,1)}, u32[]{:S(2)}) copy-start(bf16[16,512,4,64]{1,3,2,0:T(8,128)(2,1)} %get-tuple-element.10) | copy-start | bytes 12582916
  128.9 6.4 %copy-start.3 = (bf16[16,512,4,64]{1,3,2,0:T(8,128)(2,1)S(1)}, bf16[16,512,4,64]{1,3,2,0:T(8,128)(2,1)}, u32[]{:S(2)}) copy-start(bf16[16,512,4,64]{1,3,2,0:T(8,128)(2,1)} %param.4) | copy-start | bytes 12582916
  146.2 6.7 %copy-start.16 = (bf16[4,1,64,512]{3,2,1,0:T(8,128)(2,1)S(1)}, bf16[4,1,64,512]{3,2,1,0:T(8,128)(2,1)}, u32[]{:S(2)}) copy-start(bf16[4,1,64,512]{3,2,1,0:T(8,128)(2,1)} %get-tuple-element.23) | copy-start | bytes 786436
  152.9 8.1 %copy-start.15 = (bf16[4,1,64,512]{3,2,1,0:T(8,128)(2,1)S(1)}, bf16[4,1,64,512]{3,2,1,0:T(8,128)(2,1)}, u32[]{:S(2)}) copy-start(bf16[4,1,64,512]{3,2,1,0:T(8,128)(2,1)} %get-tuple-element.21) | copy-start | bytes 786436
  161.1 8.1 %copy-start.14 = (bf16[4,1,64,512]{3,2,1,0:T(8,128)(2,1)S(1)}, bf16[4,1,64,512]{3,2,1,0:T(8,128)(2,1)}, u32[]{:S(2)}) copy-start(bf16[4,1,64,512]{3,2,1,0:T(8,128)(2,1)} %get-tuple-element.20) | copy-start | bytes 786436
  169.2 8.1 %copy-start.13 = (bf16[4,1,64,512]{3,2,1,0:T(8,128)(2,1)S(1)}, bf16[4,1,64,512]{3,2,1,0:T(8,128)(2,1)}, u32[]{:S(2)}) copy-start(bf16[4,1,64,512]{3,2,1,0:T(8,128)(2,1)} %get-tuple-element.19) | copy-start | bytes 786436
  177.3 8.1 %copy-start.9 = (bf16[32,8,16,512]{3,1,2,0:T(8,128)(2,1)S(1)}, bf16[32,8,16,512]{3,1,2,0:T(8,128)(2,1)}, u32[]{:S(2)}) copy-start(bf16[32,8,16,512]{3,1,2,0:T(8,128)(2,1)} %copy.29) | copy-start | bytes 12582916
  177.3 8.1 %copy-start.12 = (bf16[4,1,64,512]{3,2,1,0:T(8,128)(2,1)S(1)}, bf16[4,1,64,512]{3,2,1,0:T(8,128)(2,1)}, u32[]{:S(2)}) copy-start(bf16[4,1,64,512]{3,2,1,0:T(8,128)(2,1)} %get-tuple-element.18) | copy-start | bytes 786436
  185.4 8.4 %copy-start.10 = (bf16[32,8,16,512]{3,1,2,0:T(8,128)(2,1)S(1)}, bf16[32,8,16,512]{3,1,2,0:T(8,128)(2,1)}, u32[]{:S(2)}) copy-start(bf16[32,8,16,512]{3,1,2,0:T(8,128)(2,1)} %copy.31) | copy-start | bytes 12582916
  201.9 8.2 %copy-start.11 = (bf16[32,8,16,512]{3,1,2,0:T(8,128)(2,1)S(1)}, bf16[32,8,16,512]{3,1,2,0:T(8,128)(2,1)}, u32[]{:S(2)}) copy-start(bf16[32,8,16,512]{3,1,2,0:T(8,128)(2,1)} %copy.30) | copy-start | bytes 12582916
  305.6 27.3 %copy-start.18 = (f32[64]{0:T(128)S(1)}, f32[64]{0:T(128)}, u32[]{:S(2)}) copy-start(f32[64]{0:T(128)} %param.6) | copy-start | bytes 772
  332.9 9.6 %copy-start.1 = (bf16[8,9,64,64]{3,2,1,0:T(8,128)(2,1)S(1)}, bf16[8,9,64,64]{3,2,1,0:T(8,128)(2,1)}, u32[]{:S(2)}) copy-start(bf16[8,9,64,64]{3,2,1,0:T(8,128)(2,1)} %param.5) | copy-start | bytes 1769476
Sparse Core Ops, SparseCore 0:
  305.7 27.1 reduce-scatter.1
where the time goes:
time: 354 us; the launch traced here: 350 us
  local copies, waits for them, and re-layouts  172 us (49%)
  matrix products  115 us (32%)
  waiting for transfers between devices  27.3 us (8%)
  other arithmetic  15.2 us (4%)
  between operations  13.9 us (4%)
  starting transfers between devices  6.17 us (2%)
    dot_general x9, matrix products, convolve(): jnp.dot(window, filters[:, tap].reshape(count * chans, filters.shape[3]),...  115 us
    unnamed x49, local copies, waits for them, and re-layouts  78.7 us
    slice x9, local copies, waits for them, and re-layouts, convolve(): padded[row_off:row_off + rows, col_off:col_off + cols]  41.2 us
    reduce_scatter x1, waiting for transfers between devices, local(): total = lax.psum_scatter(terms, 'rot', scatter_dimension=2, tiled=True)  27.3 us
    gather x2, local copies, waits for them, and re-layouts, build_filters(): picked = weight[relative[:, None, :], jnp.transpose(taps)[None, :, :]]  20.2 us
    add x1, local copies, waits for them, and re-layouts, convolve(): total + jnp.dot(window, filters[:, tap].reshape(count * chans, filters.sh...  17.4 us
    concatenate x2, other arithmetic, with_halo(): jnp.concatenate([lax.ppermute(tail, axis, [(i, (i + 1) % count) for i in...  9.84 us
  transfers between devices with their start and end apart: 3, of which 1 were waited for; matrix products, arithmetic and copies ran while one was open for 12% of the time, Pallas kernels for 0%

commit v1 on v0

v1 whole, which is shorter than its diff:
```python
import functools

import jax
import jax.numpy as jnp
import numpy as np
from jax import lax
from jax.experimental import pallas as pl
from jax.experimental.pallas import tpu as pltpu
from jax.sharding import PartitionSpec as P


def source_table():
    cycle = [5, 2, 1, 0, 3, 6, 7, 8]
    table = np.zeros((8, 9), np.int32)
    for turn in range(8):
        table[turn, 4] = 4
        for place in range(8):
            table[turn, cycle[place]] = cycle[(place - turn) % 8]
    return table


def filter_kernel(owned, orient, here_ref, weight_ref, out_ref):
    chans = weight_ref.shape[3]
    table = source_table()
    flip = here_ref[0] == 1
    for rel in range(orient):
        for tap in range(9):
            nxt = (rel + 1) % orient
            pair = jnp.concatenate([weight_ref[rel, tap], weight_ref[nxt, tap]], 0)
            turned = jnp.transpose(pair)
            for r in range(owned):
                near = int(np.argwhere(table[r] == tap)[0, 0])
                far = int(np.argwhere(table[r + owned] == tap)[0, 0])
                where = near if near == far else jnp.where(flip, far, near)
                for half in range(2):
                    for s in range(0, owned, 2):
                        if (s - r + half * owned) % orient == rel:
                            lane = (half * owned + s) * chans
                            out_ref[where, r * chans : (r + 1) * chans, lane : lane + 2 * chans] = turned


def build_filters(weight, here, owned):
    orient, taps, chans, width = weight.shape
    vmem = pl.BlockSpec(memory_space=pltpu.VMEM)
    return pl.pallas_call(
        functools.partial(filter_kernel, owned, orient),
        out_shape=jax.ShapeDtypeStruct((taps, owned * width, orient * chans), weight.dtype),
        in_specs=[pl.BlockSpec(memory_space=pltpu.SMEM), vmem],
        out_specs=vmem,
        name="filters",
    )(here, weight)


def shifted(x, step):
    cols = x.shape[1]
    place = lax.broadcasted_iota(jnp.int32, x.shape, 1) + step
    turned = pltpu.roll(x, (-step) % cols, 1)
    return jnp.where((place >= 0) & (place < cols), turned, jnp.zeros_like(turned))


def conv_kernel(
    filt_hbm, bias_ref, own_hbm, other_hbm, halo_hbm, halo_other_hbm, out_hbm,
    filt, x, out, filt_sem, in_sem, out_sem,
):
    rows = own_hbm.shape[0]
    half = own_hbm.shape[1]
    load_filt = pltpu.make_async_copy(filt_hbm, filt, filt_sem)
    load_filt.start()

    def load(j, which, src):
        lane = slice(which * half, (which + 1) * half)
        return pltpu.make_async_copy(src, x.at[j, lane], in_sem.at[which, j])

    load(0, 0, halo_hbm.at[0]).start()
    load(0, 1, halo_other_hbm.at[0]).start()

    def issue(j, carry):
        load(j + 1, 0, own_hbm.at[j]).start()
        load(j + 1, 1, other_hbm.at[j]).start()
        return carry

    lax.fori_loop(0, rows, issue, 0)
    load(rows + 1, 0, halo_hbm.at[1]).start()
    load(rows + 1, 1, halo_other_hbm.at[1]).start()

    def arrived(j):
        load(j, 0, own_hbm.at[0]).wait()
        load(j, 1, other_hbm.at[0]).wait()

    arrived(0)
    arrived(1)
    load_filt.wait()
    bias_col = bias_ref[...]

    def body(i, carry):
        for k in range(2):
            arrived(2 * i + k + 2)
        for k in range(2):
            y = 2 * i + k
            acc = None
            for a in range(3):
                line = x[y + a]
                for b in range(3):
                    term = jnp.dot(
                        filt[3 * a + b],
                        line if b == 1 else shifted(line, b - 1),
                        preferred_element_type=jnp.float32,
                    )
                    acc = term if acc is None else acc + term
            out[y] = jnp.maximum(acc + bias_col, 0.0).astype(out.dtype)
            pltpu.make_async_copy(out.at[y], out_hbm.at[y], out_sem).start()
        return carry

    lax.fori_loop(0, rows // 2, body, 0)
    pltpu.make_async_copy(out, out_hbm, out_sem).wait()


def convolve(filt, bias_col, own, other, halo, halo_other):
    rows, half, cols = own.shape
    hbm = pl.BlockSpec(memory_space=pl.ANY)
    vmem = pl.BlockSpec(memory_space=pltpu.VMEM)
    return pl.pallas_call(
        conv_kernel,
        out_shape=jax.ShapeDtypeStruct((rows, filt.shape[1], cols), jnp.bfloat16),
        in_specs=[hbm, vmem, hbm, hbm, hbm, hbm],
        out_specs=hbm,
        scratch_shapes=[
            pltpu.VMEM(filt.shape, filt.dtype),
            pltpu.VMEM((rows + 2, 2 * half, cols), own.dtype),
            pltpu.VMEM((rows, filt.shape[1], cols), jnp.bfloat16),
            pltpu.SemaphoreType.DMA,
            pltpu.SemaphoreType.DMA((2, rows + 2)),
            pltpu.SemaphoreType.DMA,
        ],
        compiler_params=pltpu.CompilerParams(vmem_limit_bytes=56 << 20),
        name="convolve",
    )(filt, bias_col, own, other, halo, halo_other)


def local(features, weight, bias):
    rows, cols, owned, chans = features.shape
    count = lax.axis_size("tile")
    swap = [(0, 1), (1, 0)]
    here = lax.axis_index("rot").astype(jnp.int32).reshape(1)
    own = jnp.transpose(features, (0, 2, 3, 1)).reshape(rows, owned * chans, cols)
    above = lax.ppermute(own[rows - 1 :], "tile", [(i, i + 1) for i in range(count - 1)])
    below = lax.ppermute(own[:1], "tile", [(i + 1, i) for i in range(count - 1)])
    other = lax.ppermute(own, "rot", swap)
    halo = jnp.concatenate([above, below], 0)
    halo_other = lax.ppermute(halo, "rot", swap)
    filt = build_filters(weight, here, owned)
    bias_col = jnp.tile(bias, owned).reshape(owned * chans, 1)
    out = convolve(filt, bias_col, own, other, halo, halo_other)
    return jnp.transpose(out.reshape(rows, owned, chans, cols), (0, 3, 1, 2))


def solution(mesh):
    spec = P(("groups", "tile"), None, "rot", None)
    return jax.shard_map(
        local,
        mesh=mesh,
        in_specs=(spec, P(), P()),
        out_specs=spec,
        check_vma=False,
    )
```

time: 354 us -> 49.9 us (0.14); the launches traced: 350 us -> 49.6 us
  local copies, waits for them, and re-layouts: 172 us -> 3.32 us
  matrix products: 115 us -> 0 us
  Pallas kernels: 0 us -> 28.4 us
  waiting for transfers between devices: 27.3 us -> 10.5 us
  other arithmetic: 15.2 us -> 0 us
  between operations: 13.9 us -> 0.05 us
    dot_general x9 -> x0, matrix products: 115 us -> none  [convolve(): jnp.dot(window, filters[:, tap].reshape(count * chans, filters.shape[3]),...]
    unnamed x49 -> x5, local copies, waits for them, and re-layouts: 78.7 us -> 0.8 us
    slice x11 -> x1, local copies, waits for them, and re-layouts: 44.2 us -> 1.06 us  [local(): own[:1]]
    pallas_call x0 -> x2, Pallas kernels: none -> 28.4 us  [the longest x1 25.1 us: convolve(): pl.pallas_call(conv_kernel, out_shape=jax.ShapeDtypeStruct((rows, filt.sh...]
    reduce_scatter x1 -> x0, waiting for transfers between devices: 27.3 us -> none  [local(): total = lax.psum_scatter(terms, 'rot', scatter_dimension=2, tiled=True)]
    gather x3 -> x0, local copies, waits for them, and re-layouts: 20.7 us -> none  [the longest x2 20.2 us: build_filters(): picked = weight[relative[:, None, :], jnp.transpose(taps)[None, :, :]]]
    add x1 -> x0, local copies, waits for them, and re-layouts: 17.4 us -> none  [convolve(): total + jnp.dot(window, filters[:, tap].reshape(count * chans, filters.sh...]
    ppermute x2 -> x4, waiting for transfers between devices: 0.01 us -> 10.5 us  [the longest x1 8.21 us: local(): lax.ppermute(own[rows - 1:], 'tile', [(i, i + 1) for i in range(count - 1)])]
  transfers between devices with their start and end apart: 3 -> 4, of which waited for: 1 -> 2; matrix products, arithmetic and copies ran while one was open for 12% -> 5% of each run, Pallas kernels for 0% -> 7%
where the time goes in v1:
time: 49.9 us; the launch traced here: 49.6 us
  Pallas kernels  28.4 us (57%)
  waiting for transfers between devices  10.5 us (21%)
  starting transfers between devices  7.39 us (15%)
  local copies, waits for them, and re-layouts  3.32 us (7%)
    pallas_call x1, Pallas kernels, convolve(): pl.pallas_call(conv_kernel, out_shape=jax.ShapeDtypeStruct((rows, filt.sh...  25.1 us
    ppermute x1, waiting for transfers between devices, local(): lax.ppermute(own[rows - 1:], 'tile', [(i, i + 1) for i in range(count - 1)])  8.21 us
    pallas_call x1, Pallas kernels, build_filters(): pl.pallas_call(functools.partial(filter_kernel, owned, orient), out_shape...  3.35 us
    ppermute x1, starting transfers between devices, local(): lax.ppermute(own[rows - 1:], 'tile', [(i, i + 1) for i in range(count - 1)])  3.15 us
    ppermute x1, starting transfers between devices, local(): lax.ppermute(own[:1], 'tile', [(i + 1, i) for i in range(count - 1)])  3.03 us
    ppermute x1, waiting for transfers between devices, local(): lax.ppermute(own[:1], 'tile', [(i + 1, i) for i in range(count - 1)])  2.23 us
    another operation x2, local copies, waits for them, and re-layouts, local(): bias_col = jnp.tile(bias, owned).reshape(owned * chans, 1)  1.44 us
    slice x1, local copies, waits for them, and re-layouts, local(): own[:1]  1.06 us
  transfers between devices with their start and end apart: 4, of which 2 were waited for; matrix products, arithmetic and copies ran while one was open for 5% of the time, Pallas kernels for 7%

profile of v1, /device:TPU:19, one launch (start us, length us, event | category | flops | bytes accessed | tf_op | source)
XLA Modules:
  0.0 49.6 jit_solution(2954950471927171912)
XLA Ops:
  0.0 0.7 %collective-permute-start = (bf16[16,256,512]{2,1,0:T(8,128)(2,1)}, bf16[16,256,512]{2,1,0:T(8,128)(2,1)}, u32[]{:S(2)}, u32[]{:S(2)}) collective-permute-start(bf16[16,256,512]{2,1,0:T(8,128)(2,1)} %bitcast.9), channel_id=1, source_target_pairs={{0,1},{1,0},{2,3},{3,2},{4,5},{5,4},{6,7},{7,6},{8,9},{9,8},{10,11... | collective-permute-start | bytes 12582920 | tf_op jit(solution)/shard_map/ppermute | solution.py:148
  0.7 1.1 %fusion = (bf16[1,4,64,512]{3,2,1,0:T(8,128)(2,1)S(1)}, bf16[1,4,64,512]{3,2,1,0:T(8,128)(2,1)S(1)}) fusion(bf16[16,4,64,512]{3,2,1,0:T(8,128)(2,1)} %bitcast.10), kind=kLoop, calls=%fused_computation.2 | loop fusion | bytes 1048576 | tf_op jit(solution)/shard_map/slice | solution.py:147
  1.7 3.1 %collective-permute-start.1 = (bf16[1,256,512]{2,1,0:T(8,128)(2,1)S(1)}, bf16[1,256,512]{2,1,0:T(8,128)(2,1)S(1)}, u32[]{:S(2)}, u32[]{:S(2)}) collective-permute-start(bf16[1,256,512]{2,1,0:T(8,128)(2,1)S(1)} %bitcast.13), channel_id=1, source_target_pairs={{0,2},{2,4},{4,6},{6,8},{8,10},{10,12},{12,14},{1,3},{3,5},{5,7},{... | collective-permute-start | bytes 786440 | tf_op jit(solution)/shard_map/ppermute | solution.py:146
  4.9 3.0 %collective-permute-start.2 = (bf16[1,256,512]{2,1,0:T(8,128)(2,1)S(1)}, bf16[1,256,512]{2,1,0:T(8,128)(2,1)S(1)}, u32[]{:S(2)}, u32[]{:S(2)}) collective-permute-start(bf16[1,256,512]{2,1,0:T(8,128)(2,1)S(1)} %bitcast.12), channel_id=1, source_target_pairs={{2,0},{4,2},{6,4},{8,6},{10,8},{12,10},{14,12},{3,1},{5,3},{7,5},{... | collective-permute-start | bytes 786440 | tf_op jit(solution)/shard_map/ppermute | solution.py:147
  7.9 8.2 %collective-permute-done.1 = bf16[1,256,512]{2,1,0:T(8,128)(2,1)S(1)} collective-permute-done((bf16[1,256,512]{2,1,0:T(8,128)(2,1)S(1)}, bf16[1,256,512]{2,1,0:T(8,128)(2,1)S(1)}, u32[]{:S(2)}, u32[]{:S(2)}) %collective-permute-start.1) | collective-permute-done | bytes 262176 | tf_op jit(solution)/shard_map/ppermute | solution.py:146
  16.2 2.2 %collective-permute-done.2 = bf16[1,256,512]{2,1,0:T(8,128)(2,1)S(1)} collective-permute-done((bf16[1,256,512]{2,1,0:T(8,128)(2,1)S(1)}, bf16[1,256,512]{2,1,0:T(8,128)(2,1)S(1)}, u32[]{:S(2)}, u32[]{:S(2)}) %collective-permute-start.2) | collective-permute-done | bytes 262176 | tf_op jit(solution)/shard_map/ppermute | solution.py:147
  18.4 0.0 copy-start
  18.4 0.5 %collective-permute-start.3 = (bf16[2,256,512]{2,1,0:T(8,128)(2,1)S(1)}, bf16[2,256,512]{2,1,0:T(8,128)(2,1)S(1)}, u32[]{:S(2)}, u32[]{:S(2)}) collective-permute-start(bf16[2,256,512]{2,1,0:T(8,128)(2,1)S(1)} %constant_dynamic-update-slice_fusion.halo_hbm), channel_id=1, source_target_pairs={{0,1},{1,0},{2,3},{3,2},{4,5},{5,4},{6,7},{7,6},{8,9},{9,8},{10,11... | collective-permute-start | bytes 1572872 | tf_op jit(solution)/shard_map/ppermute | solution.py:150
  19.0 0.7 %tile.2 = f32[4,64]{1,0:T(4,128)S(1)} broadcast(f32[64]{0:T(128)} %param.5), dimensions={1} | broadcast | bytes 1280 | tf_op jit(solution)/shard_map/tile | solution.py:152
  19.6 0.8 %reshape_tile.4.bias_ref = f32[256,1]{1,0:T(8,128)} reshape(f32[4,64]{1,0:T(4,128)S(1)} %tile.2) | data formatting | bytes 2048 | tf_op jit(solution)/shard_map/reshape;tile | solution.py:152
  20.4 3.3 %filters.1.filt_hbm = bf16[9,256,512]{2,1,0:T(8,128)(2,1)} custom-call(s32[1]{0:T(128)} %bitcast.here_ref, bf16[8,9,64,64]{3,2,1,0:T(8,128)(2,1)} %weight_ref.1), custom_call_target="tpu_custom_call" | custom-call | tf_op jit(solution)/shard_map/filters/pallas_call | solution.py:45
  23.8 0.0 collective-permute-done.3.halo_other_hbm
  23.8 0.0 copy-start.1
  23.8 0.0 collective-permute-done.other_hbm
  23.8 0.0 copy-done
  23.8 0.8 %copy-done.1 = bf16[2,256,512]{2,1,0:T(8,128)(2,1)} copy-done((bf16[2,256,512]{2,1,0:T(8,128)(2,1)}, bf16[2,256,512]{2,1,0:T(8,128)(2,1)S(1)}, u32[]{:S(2)}) %copy-start.1) | copy-done | bytes 524312
  24.6 25.1 %convolve.1 = bf16[16,256,512]{2,1,0:T(8,128)(2,1)} custom-call(bf16[9,256,512]{2,1,0:T(8,128)(2,1)} %filters.1.filt_hbm, f32[256,1]{1,0:T(8,128)} %reshape_tile.4.bias_ref, bf16[16,256,512]{2,1,0:T(8,128)(2,1)} %bitcast.11, bf16[16,256,512]{2,1,0:T(8,128)(2,1)} %collective-permute-done.other_hbm, bf16[2,256,512]{2,1,0:T(8,128)(2,1)} %copy-done, ...), custom_call_target="tpu_custom_call" | custom-call | tf_op jit(solution)/shard_map/convolve/pallas_call | solution.py:122
  (2 shorter events, 0.0 us)
Async XLA Ops:
  0.0 23.8 %collective-permute-start = (bf16[16,256,512]{2,1,0:T(8,128)(2,1)}, bf16[16,256,512]{2,1,0:T(8,128)(2,1)}, u32[]{:S(2)}, u32[]{:S(2)}) collective-permute-start(bf16[16,256,512]{2,1,0:T(8,128)(2,1)} %bitcast.9), channel_id=1, source_target_pairs={{0,1},{1,0},{2,3},{3,2},{4,5},{5,4},{6,7},{7,6},{8,9},{9,8},{10,11... | collective-permute-start | bytes 12582920 | tf_op jit(solution)/shard_map/ppermute | solution.py:148
  1.7 14.4 %collective-permute-start.1 = (bf16[1,256,512]{2,1,0:T(8,128)(2,1)S(1)}, bf16[1,256,512]{2,1,0:T(8,128)(2,1)S(1)}, u32[]{:S(2)}, u32[]{:S(2)}) collective-permute-start(bf16[1,256,512]{2,1,0:T(8,128)(2,1)S(1)} %bitcast.13), channel_id=1, source_target_pairs={{0,2},{2,4},{4,6},{6,8},{8,10},{10,12},{12,14},{1,3},{3,5},{5,7},{... | collective-permute-start | bytes 786440 | tf_op jit(solution)/shard_map/ppermute | solution.py:146
  4.9 13.5 %collective-permute-start.2 = (bf16[1,256,512]{2,1,0:T(8,128)(2,1)S(1)}, bf16[1,256,512]{2,1,0:T(8,128)(2,1)S(1)}, u32[]{:S(2)}, u32[]{:S(2)}) collective-permute-start(bf16[1,256,512]{2,1,0:T(8,128)(2,1)S(1)} %bitcast.12), channel_id=1, source_target_pairs={{2,0},{4,2},{6,4},{8,6},{10,8},{12,10},{14,12},{3,1},{5,3},{7,5},{... | collective-permute-start | bytes 786440 | tf_op jit(solution)/shard_map/ppermute | solution.py:147
  18.4 5.3 %copy-start = (bf16[2,256,512]{2,1,0:T(8,128)(2,1)}, bf16[2,256,512]{2,1,0:T(8,128)(2,1)S(1)}, u32[]{:S(2)}) copy-start(bf16[2,256,512]{2,1,0:T(8,128)(2,1)S(1)} %constant_dynamic-update-slice_fusion.halo_hbm) | copy-start | bytes 1572868
  18.4 5.3 %collective-permute-start.3 = (bf16[2,256,512]{2,1,0:T(8,128)(2,1)S(1)}, bf16[2,256,512]{2,1,0:T(8,128)(2,1)S(1)}, u32[]{:S(2)}, u32[]{:S(2)}) collective-permute-start(bf16[2,256,512]{2,1,0:T(8,128)(2,1)S(1)} %constant_dynamic-update-slice_fusion.halo_hbm), channel_id=1, source_target_pairs={{0,1},{1,0},{2,3},{3,2},{4,5},{5,4},{6,7},{7,6},{8,9},{9,8},{10,11... | collective-permute-start | bytes 1572872 | tf_op jit(solution)/shard_map/ppermute | solution.py:150
  23.8 0.8 %copy-start.1 = (bf16[2,256,512]{2,1,0:T(8,128)(2,1)}, bf16[2,256,512]{2,1,0:T(8,128)(2,1)S(1)}, u32[]{:S(2)}) copy-start(bf16[2,256,512]{2,1,0:T(8,128)(2,1)S(1)} %collective-permute-done.3.halo_other_hbm) | copy-start | bytes 1572868

commit v2 on v1

v2 whole, which is shorter than its diff:
```python
import functools

import jax
import jax.numpy as jnp
import numpy as np
from jax import lax
from jax.experimental import pallas as pl
from jax.experimental.pallas import tpu as pltpu
from jax.sharding import PartitionSpec as P

VMEM = pl.BlockSpec(memory_space=pltpu.VMEM)
HBM = pl.BlockSpec(memory_space=pltpu.HBM)


def source_table():
    cycle = [5, 2, 1, 0, 3, 6, 7, 8]
    table = np.zeros((8, 9), np.int32)
    for turn in range(8):
        table[turn, 4] = 4
        for place in range(8):
            table[turn, cycle[place]] = cycle[(place - turn) % 8]
    return table


def filters_kernel(owned, orient, weight_ref, bias_ref, filt_ref, column_ref):
    chans = weight_ref.shape[3]
    table = source_table()
    flip = lax.axis_index("rot") == 1
    for rel in range(orient):
        for tap in range(9):
            pair = jnp.concatenate([weight_ref[rel, tap], weight_ref[(rel + 1) % orient, tap]], 0)
            turned = jnp.transpose(pair)
            for r in range(owned):
                here = int(np.argwhere(table[r] == tap)[0, 0])
                there = int(np.argwhere(table[r + owned] == tap)[0, 0])
                where = here if here == there else jnp.where(flip, there, here)
                for half in range(2):
                    for s in range(0, owned, 2):
                        if (s - r + half * owned) % orient == rel:
                            lane = (half * owned + s) * chans
                            filt_ref[where, r * chans : (r + 1) * chans, lane : lane + 2 * chans] = turned
    wide = jnp.broadcast_to(bias_ref[...], (128, chans))
    column_ref[...] = jnp.concatenate([jnp.transpose(wide)] * owned, 0)


def build_filters(weight, bias, owned):
    orient, taps, chans, width = weight.shape
    return pl.pallas_call(
        functools.partial(filters_kernel, owned, orient),
        out_shape=(
            jax.ShapeDtypeStruct((taps, owned * width, orient * chans), weight.dtype),
            jax.ShapeDtypeStruct((owned * width, 128), jnp.float32),
        ),
        in_specs=[VMEM, VMEM],
        out_specs=(VMEM, VMEM),
        compiler_params=pltpu.CompilerParams(vmem_limit_bytes=12 << 20),
        name="filters",
    )(weight, bias)


def pick_kernel(own, near, far, near_sem, far_sem):
    rows = own.shape[0]
    even = lax.rem(lax.axis_index("tile"), 2) == 0
    first = jnp.where(even, rows - 1, 0)
    send_near = pltpu.make_async_copy(own.at[pl.ds(first, 1)], near, near_sem)
    send_far = pltpu.make_async_copy(own.at[pl.ds(rows - 1 - first, 1)], far, far_sem)
    send_near.start()
    send_far.start()
    send_near.wait()
    send_far.wait()


def pick_edges(own):
    edge = jax.ShapeDtypeStruct((1,) + own.shape[1:], own.dtype)
    return pl.pallas_call(
        pick_kernel,
        out_shape=(edge, edge),
        in_specs=[HBM],
        out_specs=(VMEM, VMEM),
        scratch_shapes=[pltpu.SemaphoreType.DMA, pltpu.SemaphoreType.DMA],
        compiler_params=pltpu.CompilerParams(vmem_limit_bytes=4 << 20),
        name="pick",
    )(pltpu.with_memory_space_constraint(own, pltpu.HBM))


def shifted(x, step):
    cols = x.shape[1]
    place = lax.broadcasted_iota(jnp.int32, x.shape, 1) + step
    turned = pltpu.roll(x, (-step) % cols, 1)
    return jnp.where((place >= 0) & (place < cols), turned, jnp.zeros_like(turned))


def row_sums(filt, lines, column):
    half = filt.shape[2] // 2
    acc = None
    for b in (1, 0, 2):
        for a, line in enumerate(lines):
            for which, part in enumerate(line):
                term = jnp.dot(
                    filt[3 * a + b, :, which * half : (which + 1) * half],
                    part if b == 1 else shifted(part, b - 1),
                    preferred_element_type=jnp.float32,
                )
                acc = term if acc is None else acc + term
    wide = jnp.concatenate([column] * (acc.shape[1] // column.shape[1]), 1)
    return jnp.maximum(acc + wide, 0.0).astype(jnp.bfloat16)


def inner_kernel(first, last, filt, column, own, other, *rest):
    out_hbm, out, out_sem = rest[-3:]
    for y in range(first, last):
        lines = [(own[y + a - 1], other[y + a - 1]) for a in range(3)]
        out[y - first] = row_sums(filt, lines, column[...])
        pltpu.make_async_copy(out.at[y - first], out_hbm.at[y], out_sem).start()
    pltpu.make_async_copy(out, out_hbm.at[pl.ds(first, last - first)], out_sem).wait()


def inner(first, last, filt, column, own, other, partial=None):
    rows, half, cols = own.shape
    count = last - first
    flops = 2 * count * cols * filt.shape[0] * filt.shape[1] * filt.shape[2]
    extra = [] if partial is None else [partial]
    return pl.pallas_call(
        functools.partial(inner_kernel, first, last),
        out_shape=jax.ShapeDtypeStruct((rows, filt.shape[1], cols), jnp.bfloat16),
        in_specs=[VMEM] * 4 + [HBM] * len(extra),
        out_specs=HBM,
        scratch_shapes=[
            pltpu.VMEM((count, filt.shape[1], cols), jnp.bfloat16),
            pltpu.SemaphoreType.DMA,
        ],
        input_output_aliases={4: 0} if extra else {},
        compiler_params=pltpu.CompilerParams(vmem_limit_bytes=20 << 20),
        cost_estimate=pl.CostEstimate(flops=flops, bytes_accessed=count * half * cols * 6, transcendentals=0),
        name="inner",
    )(filt, column, own, other, *extra)


def edge_kernel(filt, column, own, other, near_own, near_other, far_own, far_other, partial, out_hbm, out, out_sem):
    rows = own.shape[0]
    even = lax.rem(lax.axis_index("tile"), 2) == 0
    pairs = ((near_own[0], far_own[0]), (near_other[0], far_other[0]))
    above = [jnp.where(even, far, near) for near, far in pairs]
    below = [jnp.where(even, near, far) for near, far in pairs]
    sends = []
    for k, y in enumerate((0, rows - 1)):
        body = [(own[j], other[j]) for j in ((0, 1), (rows - 2, rows - 1))[k]]
        out[k] = row_sums(filt, [above] + body if k == 0 else body + [below], column[...])
        sends.append(pltpu.make_async_copy(out.at[k], out_hbm.at[y], out_sem.at[k]))
        sends[-1].start()
    for send in sends:
        send.wait()


def edges(filt, column, own, other, near_own, near_other, far_own, far_other, partial):
    rows, half, cols = own.shape
    return pl.pallas_call(
        edge_kernel,
        out_shape=jax.ShapeDtypeStruct(partial.shape, partial.dtype),
        in_specs=[VMEM] * 8 + [HBM],
        out_specs=HBM,
        scratch_shapes=[
            pltpu.VMEM((2, filt.shape[1], cols), jnp.bfloat16),
            pltpu.SemaphoreType.DMA((2,)),
        ],
        input_output_aliases={8: 0},
        compiler_params=pltpu.CompilerParams(vmem_limit_bytes=20 << 20),
        name="edges",
    )(filt, column, own, other, near_own, near_other, far_own, far_other, partial)


def local(features, weight, bias):
    rows, cols, owned, chans = features.shape
    count = lax.axis_size("tile")
    swap = [(0, 1), (1, 0)]
    own = jnp.transpose(features, (0, 2, 3, 1)).reshape(rows, owned * chans, cols)
    other = lax.ppermute(own, "rot", swap)
    near, far = pick_edges(own)

    def pairs(start):
        return [p for k in range(start, count - 1, 2) for p in ((k, k + 1), (k + 1, k))]

    near_own = lax.ppermute(near, "tile", pairs(0))
    far_own = lax.ppermute(far, "tile", pairs(1))
    filt, column = build_filters(weight, bias.reshape(1, chans), owned)
    split = rows // 2
    out = inner(1, split, filt, column, own, other)
    near_own, far_own, out = lax.optimization_barrier((near_own, far_own, out))
    near_other = lax.ppermute(near_own, "rot", swap)
    far_other = lax.ppermute(far_own, "rot", swap)
    out = inner(split, rows - 1, filt, column, own, other, out)
    out = edges(filt, column, own, other, near_own, near_other, far_own, far_other, out)
    return jnp.transpose(out.reshape(rows, owned, chans, cols), (0, 3, 1, 2))


def solution(mesh):
    spec = P(("groups", "tile"), None, "rot", None)
    return jax.shard_map(
        local,
        mesh=mesh,
        in_specs=(spec, P(), P()),
        out_specs=spec,
        check_vma=False,
    )
```

time: 49.9 us -> 31.7 us (0.64)
  the two profiles are of different devices: /device:TPU:19 before, /device:TPU:7 now
where the time goes in v2:
time: 31.7 us; the launch traced here: 31.6 us
  Pallas kernels  24.1 us (76%)
  starting transfers between devices  5.89 us (19%)
  local copies, waits for them, and re-layouts  1.27 us (4%)
    pallas_call x2, Pallas kernels, inner(): pl.pallas_call(functools.partial(inner_kernel, first, last), out_shape=ja...  19 us
    ppermute x1, starting transfers between devices, local(): far_own = lax.ppermute(far, 'tile', pairs(1))  4.15 us
    pallas_call x1, Pallas kernels, edges(): pl.pallas_call(edge_kernel, out_shape=jax.ShapeDtypeStruct(partial.shape,...  3.34 us
    unnamed x6, local copies, waits for them, and re-layouts  1.27 us
    pallas_call x1, Pallas kernels, pick_edges(): pl.pallas_call(pick_kernel, out_shape=(edge, edge), in_specs=[HBM], out_s...  1.15 us
    ppermute x1, starting transfers between devices, local(): near_other = lax.ppermute(near_own, 'rot', swap)  0.69 us
    ppermute x1, starting transfers between devices, local(): other = lax.ppermute(own, 'rot', swap)  0.68 us
    pallas_call x1, Pallas kernels, build_filters(): pl.pallas_call(functools.partial(filters_kernel, owned, orient), out_shap...  0.67 us
  transfers between devices with their start and end apart: 5, of which 0 were waited for; matrix products, arithmetic and copies ran while one was open for 0% of the time, Pallas kernels for 66%

profile of v2, /device:TPU:7, one launch (start us, length us, event | category | flops | bytes accessed | tf_op | source)
XLA Modules:
  0.0 31.6 jit_solution(8063962656417947525)
XLA Ops:
  0.0 0.0 copy-start
  0.0 0.0 copy-start.2
  0.0 0.7 %collective-permute-start = (bf16[16,256,512]{2,1,0:T(8,128)(2,1)}, bf16[16,256,512]{2,1,0:T(8,128)(2,1)S(1)}, u32[]{:S(2)}, u32[]{:S(2)}) collective-permute-start(bf16[16,256,512]{2,1,0:T(8,128)(2,1)} %bitcast.7), channel_id=1, source_target_pairs={{0,1},{1,0},{2,3},{3,2},{4,5},{5,4},{6,7},{7,6},{8,9},{9,8},{10,11... | collective-permute-start | bytes 12582920 | tf_op jit(solution)/shard_map/ppermute | solution.py:177
  0.7 1.2 %pick.1 = (bf16[1,256,512]{2,1,0:T(8,128)(2,1)S(1)}, bf16[1,256,512]{2,1,0:T(8,128)(2,1)S(1)}) custom-call(bf16[16,256,512]{2,1,0:T(8,128)(2,1)} %bitcast.8), custom_call_target="tpu_custom_call" | custom-call | tf_op jit(solution)/shard_map/pick/pallas_call | solution.py:75
  1.8 0.3 collective-permute-start.1
  2.1 4.1 %collective-permute-start.2 = (bf16[1,256,512]{2,1,0:T(8,128)(2,1)S(1)}, bf16[1,256,512]{2,1,0:T(8,128)(2,1)S(1)}, u32[]{:S(2)}, u32[]{:S(2)}) collective-permute-start(bf16[1,256,512]{2,1,0:T(8,128)(2,1)S(1)} %get-tuple-element.15), channel_id=1, source_target_pairs={{2,4},{4,2},{6,8},{8,6},{10,12},{12,10},{3,5},{5,3},{7,9},{9,7},{1... | collective-permute-start | bytes 786440 | tf_op jit(solution)/shard_map/ppermute | solution.py:184
  6.3 0.0 copy-done.2
  6.3 0.0 copy-start.1
  6.3 1.3 %copy-done.1 = bf16[8,9,64,64]{3,2,1,0:T(8,128)(2,1)S(1)} copy-done((bf16[8,9,64,64]{3,2,1,0:T(8,128)(2,1)S(1)}, bf16[8,9,64,64]{3,2,1,0:T(8,128)(2,1)}, u32[]{:S(2)}) %copy-start.1) | copy-done | bytes 589848
  7.6 0.7 %filters.1 = (bf16[9,256,512]{2,1,0:T(8,128)(2,1)S(1)}, f32[256,128]{1,0:T(8,128)S(1)}) custom-call(bf16[8,9,64,64]{3,2,1,0:T(8,128)(2,1)S(1)} %copy-done.1, f32[1,64]{1,0:T(1,128)S(1)} %bitcast.12), custom_call_target="tpu_custom_call" | custom-call | tf_op jit(solution)/shard_map/filters/pallas_call | solution.py:48
  8.3 0.0 collective-permute-done.other
  8.3 0.0 copy-done
  8.3 9.4 %inner.2.rest_0_ = bf16[16,256,512]{2,1,0:T(8,128)(2,1)} custom-call(bf16[9,256,512]{2,1,0:T(8,128)(2,1)S(1)} %get-tuple-element.12.filt, f32[256,128]{1,0:T(8,128)S(1)} %get-tuple-element.13.column, bf16[16,256,512]{2,1,0:T(8,128)(2,1)S(1)} %bitcast.9, bf16[16,256,512]{2,1,0:T(8,128)(2,1)S(1)} %collective-permute-done.other), custom_call_target="tpu_custom_call" | custom-call | flops 8455716864 | bytes 5505024 | tf_op jit(solution)/shard_map/inner/pallas_call | solution.py:123
  17.7 0.0 collective-permute-done.1.near_own
  17.7 0.0 collective-permute-done.2.far_own
  17.7 0.7 %collective-permute-start.3 = (bf16[1,256,512]{2,1,0:T(8,128)(2,1)S(1)}, bf16[1,256,512]{2,1,0:T(8,128)(2,1)S(1)}, u32[]{:S(2)}, u32[]{:S(2)}) collective-permute-start(bf16[1,256,512]{2,1,0:T(8,128)(2,1)S(1)} %collective-permute-done.1.near_own), channel_id=1, source_target_pairs={{0,1},{1,0},{2,3},{3,2},{4,5},{5,4},{6,7},{7,6},{8,9},{9,8},{10,11... | collective-permute-start | bytes 786440 | tf_op jit(solution)/shard_map/ppermute | solution.py:189
  18.4 0.1 collective-permute-start.4
  18.5 9.6 %inner.3.partial = bf16[16,256,512]{2,1,0:T(8,128)(2,1)} custom-call(bf16[9,256,512]{2,1,0:T(8,128)(2,1)S(1)} %get-tuple-element.12.filt, f32[256,128]{1,0:T(8,128)S(1)} %get-tuple-element.13.column, bf16[16,256,512]{2,1,0:T(8,128)(2,1)S(1)} %bitcast.10, bf16[16,256,512]{2,1,0:T(8,128)(2,1)S(1)} %collective-permute-done.other, ...), custom_call_target="tpu_custom_call", output_to_operand_aliasing={{}: (4, {})} | custom-call | flops 8455716864 | bytes 5505024 | tf_op jit(solution)/shard_map/inner/pallas_call | solution.py:123
  28.1 0.0 collective-permute-done.3.near_other
  28.1 0.0 collective-permute-done.4.far_other
  28.1 3.3 %edges.1 = bf16[16,256,512]{2,1,0:T(8,128)(2,1)} custom-call(bf16[9,256,512]{2,1,0:T(8,128)(2,1)S(1)} %get-tuple-element.12.filt, f32[256,128]{1,0:T(8,128)S(1)} %get-tuple-element.13.column, bf16[16,256,512]{2,1,0:T(8,128)(2,1)S(1)} %bitcast.11, bf16[16,256,512]{2,1,0:T(8,128)(2,1)S(1)} %collective-permute-done.other, ...), custom_call_target="tpu_custom_call", output_to_operand_aliasing={{}: (8, {})} | custom-call | tf_op jit(solution)/shard_map/edges/pallas_call | solution.py:157
Async XLA Ops:
  0.0 8.3 %copy-start = (bf16[16,512,4,64]{1,3,2,0:T(8,128)(2,1)S(1)}, bf16[16,512,4,64]{1,3,2,0:T(8,128)(2,1)}, u32[]{:S(2)}) copy-start(bf16[16,512,4,64]{1,3,2,0:T(8,128)(2,1)} %param.3) | copy-start | bytes 12582916
  0.0 6.3 %copy-start.2 = (f32[64]{0:T(128)S(1)}, f32[64]{0:T(128)}, u32[]{:S(2)}) copy-start(f32[64]{0:T(128)} %param.5) | copy-start | bytes 772
  0.0 8.2 %collective-permute-start = (bf16[16,256,512]{2,1,0:T(8,128)(2,1)}, bf16[16,256,512]{2,1,0:T(8,128)(2,1)S(1)}, u32[]{:S(2)}, u32[]{:S(2)}) collective-permute-start(bf16[16,256,512]{2,1,0:T(8,128)(2,1)} %bitcast.7), channel_id=1, source_target_pairs={{0,1},{1,0},{2,3},{3,2},{4,5},{5,4},{6,7},{7,6},{8,9},{9,8},{10,11... | collective-permute-start | bytes 12582920 | tf_op jit(solution)/shard_map/ppermute | solution.py:177
  1.8 15.8 %collective-permute-start.1 = (bf16[1,256,512]{2,1,0:T(8,128)(2,1)S(1)}, bf16[1,256,512]{2,1,0:T(8,128)(2,1)S(1)}, u32[]{:S(2)}, u32[]{:S(2)}) collective-permute-start(bf16[1,256,512]{2,1,0:T(8,128)(2,1)S(1)} %get-tuple-element.14), channel_id=1, source_target_pairs={{0,2},{2,0},{4,6},{6,4},{8,10},{10,8},{12,14},{14,12},{1,3},{3,1},... | collective-permute-start | bytes 786440 | tf_op jit(solution)/shard_map/ppermute | solution.py:183
  2.1 15.5 %collective-permute-start.2 = (bf16[1,256,512]{2,1,0:T(8,128)(2,1)S(1)}, bf16[1,256,512]{2,1,0:T(8,128)(2,1)S(1)}, u32[]{:S(2)}, u32[]{:S(2)}) collective-permute-start(bf16[1,256,512]{2,1,0:T(8,128)(2,1)S(1)} %get-tuple-element.15), channel_id=1, source_target_pairs={{2,4},{4,2},{6,8},{8,6},{10,12},{12,10},{3,5},{5,3},{7,9},{9,7},{1... | collective-permute-start | bytes 786440 | tf_op jit(solution)/shard_map/ppermute | solution.py:184
  6.3 1.3 %copy-start.1 = (bf16[8,9,64,64]{3,2,1,0:T(8,128)(2,1)S(1)}, bf16[8,9,64,64]{3,2,1,0:T(8,128)(2,1)}, u32[]{:S(2)}) copy-start(bf16[8,9,64,64]{3,2,1,0:T(8,128)(2,1)} %weight_ref.1) | copy-start | bytes 1769476
  17.7 10.4 %collective-permute-start.3 = (bf16[1,256,512]{2,1,0:T(8,128)(2,1)S(1)}, bf16[1,256,512]{2,1,0:T(8,128)(2,1)S(1)}, u32[]{:S(2)}, u32[]{:S(2)}) collective-permute-start(bf16[1,256,512]{2,1,0:T(8,128)(2,1)S(1)} %collective-permute-done.1.near_own), channel_id=1, source_target_pairs={{0,1},{1,0},{2,3},{3,2},{4,5},{5,4},{6,7},{7,6},{8,9},{9,8},{10,11... | collective-permute-start | bytes 786440 | tf_op jit(solution)/shard_map/ppermute | solution.py:189
  18.4 9.7 %collective-permute-start.4 = (bf16[1,256,512]{2,1,0:T(8,128)(2,1)S(1)}, bf16[1,256,512]{2,1,0:T(8,128)(2,1)S(1)}, u32[]{:S(2)}, u32[]{:S(2)}) collective-permute-start(bf16[1,256,512]{2,1,0:T(8,128)(2,1)S(1)} %collective-permute-done.2.far_own), channel_id=1, source_target_pairs={{0,1},{1,0},{2,3},{3,2},{4,5},{5,4},{6,7},{7,6},{8,9},{9,8},{10,11... | collective-permute-start | bytes 786440 | tf_op jit(solution)/shard_map/ppermute | solution.py:190

commit v3 on v2

v3 whole, which is shorter than its diff:
```python
import functools

import jax
import jax.numpy as jnp
import numpy as np
from jax import lax
from jax.experimental import pallas as pl
from jax.experimental.pallas import tpu as pltpu
from jax.sharding import PartitionSpec as P

VMEM = pl.BlockSpec(memory_space=pltpu.VMEM)
HBM = pl.BlockSpec(memory_space=pltpu.HBM)


def source_table():
    cycle = [5, 2, 1, 0, 3, 6, 7, 8]
    table = np.zeros((8, 9), np.int32)
    for turn in range(8):
        table[turn, 4] = 4
        for place in range(8):
            table[turn, cycle[place]] = cycle[(place - turn) % 8]
    return table


def filters_kernel(owned, orient, weight_ref, bias_ref, filt_ref, column_ref):
    chans = weight_ref.shape[3]
    table = source_table()
    flip = lax.axis_index("rot") == 1
    for rel in range(orient):
        for tap in range(9):
            pair = jnp.concatenate([weight_ref[rel, tap], weight_ref[(rel + 1) % orient, tap]], 0)
            turned = jnp.transpose(pair)
            for r in range(owned):
                here = int(np.argwhere(table[r] == tap)[0, 0])
                there = int(np.argwhere(table[r + owned] == tap)[0, 0])
                where = here if here == there else jnp.where(flip, there, here)
                for half in range(2):
                    for s in range(0, owned, 2):
                        if (s - r + half * owned) % orient == rel:
                            lane = (half * owned + s) * chans
                            filt_ref[where, r * chans : (r + 1) * chans, lane : lane + 2 * chans] = turned
    wide = jnp.broadcast_to(bias_ref[...], (128, chans))
    column_ref[...] = jnp.concatenate([jnp.transpose(wide)] * owned, 0)


def build_filters(weight, bias, owned):
    orient, taps, chans, width = weight.shape
    return pl.pallas_call(
        functools.partial(filters_kernel, owned, orient),
        out_shape=(
            jax.ShapeDtypeStruct((taps, owned * width, orient * chans), weight.dtype),
            jax.ShapeDtypeStruct((owned * width, 128), jnp.float32),
        ),
        in_specs=[VMEM, VMEM],
        out_specs=(VMEM, VMEM),
        compiler_params=pltpu.CompilerParams(vmem_limit_bytes=12 << 20),
        name="filters",
    )(weight, bias)


def pick_kernel(own, weight_hbm, near, far, weight, sems):
    rows = own.shape[0]
    even = lax.rem(lax.axis_index("tile"), 2) == 0
    first = jnp.where(even, rows - 1, 0)
    copies = [
        pltpu.make_async_copy(own.at[pl.ds(first, 1)], near, sems.at[0]),
        pltpu.make_async_copy(own.at[pl.ds(rows - 1 - first, 1)], far, sems.at[1]),
        pltpu.make_async_copy(weight_hbm, weight, sems.at[2]),
    ]
    for copy in copies:
        copy.start()
    for copy in copies:
        copy.wait()


def pick_edges(own, weight):
    edge = jax.ShapeDtypeStruct((1,) + own.shape[1:], own.dtype)
    return pl.pallas_call(
        pick_kernel,
        out_shape=(edge, edge, jax.ShapeDtypeStruct(weight.shape, weight.dtype)),
        in_specs=[HBM, HBM],
        out_specs=(VMEM, VMEM, VMEM),
        scratch_shapes=[pltpu.SemaphoreType.DMA((3,))],
        compiler_params=pltpu.CompilerParams(vmem_limit_bytes=8 << 20),
        name="pick",
    )(*(pltpu.with_memory_space_constraint(array, pltpu.HBM) for array in (own, weight)))


def shifted(x, step):
    cols = x.shape[1]
    place = lax.broadcasted_iota(jnp.int32, x.shape, 1) + step
    turned = pltpu.roll(x, (-step) % cols, 1)
    return jnp.where((place >= 0) & (place < cols), turned, jnp.zeros_like(turned))


def row_sums(filt, lines, column):
    half = filt.shape[2] // 2
    acc = None
    for b in (1, 0, 2):
        for a, line in enumerate(lines):
            for which, part in enumerate(line):
                term = jnp.dot(
                    filt[3 * a + b, :, which * half : (which + 1) * half],
                    part if b == 1 else shifted(part, b - 1),
                    preferred_element_type=jnp.float32,
                )
                acc = term if acc is None else acc + term
    wide = jnp.concatenate([column] * (acc.shape[1] // column.shape[1]), 1)
    return jnp.maximum(acc + wide, 0.0).astype(jnp.bfloat16)


def send(held, out_hbm, start, sem):
    return pltpu.make_async_copy(held, out_hbm.at[pl.ds(start, held.shape[0])], sem)


def first_kernel(filt, column, own, other, held):
    for k in range(held.shape[0]):
        lines = [(own[k + a], other[k + a]) for a in range(3)]
        held[k] = row_sums(filt, lines, column[...])


def second_kernel(filt, column, own, other, done, out_hbm, held, sem):
    copy = send(done, out_hbm, 1, sem)
    copy.start()
    start = 1 + done.shape[0]
    for k in range(held.shape[0]):
        lines = [(own[start + k + a - 1], other[start + k + a - 1]) for a in range(3)]
        held[k] = row_sums(filt, lines, column[...])
    copy.wait()


def last_kernel(
    filt, column, own, other, near_own, near_other, far_own, far_other, done, partial, out_hbm, out, sem, out_sem
):
    rows = own.shape[0]
    copies = [send(done, out_hbm, rows - 1 - done.shape[0], sem)]
    copies[0].start()
    even = lax.rem(lax.axis_index("tile"), 2) == 0
    pairs = ((near_own[0], far_own[0]), (near_other[0], far_other[0]))
    above = [jnp.where(even, far, near) for near, far in pairs]
    below = [jnp.where(even, near, far) for near, far in pairs]
    for k, y in enumerate((0, rows - 1)):
        body = [(own[j], other[j]) for j in ((0, 1), (rows - 2, rows - 1))[k]]
        out[k] = row_sums(filt, [above] + body if k == 0 else body + [below], column[...])
        copies.append(pltpu.make_async_copy(out.at[k], out_hbm.at[y], out_sem.at[k]))
        copies[-1].start()
    for copy in copies:
        copy.wait()


def call(kernel, name, shapes, inputs, scratch, aliases, count):
    filt, column, own, other = inputs[:4]
    rows, half, cols = own.shape
    flops = 2 * count * cols * filt.shape[0] * filt.shape[1] * filt.shape[2]
    return pl.pallas_call(
        kernel,
        out_shape=shapes,
        in_specs=[VMEM] * (len(inputs) - len(aliases)) + [HBM] * len(aliases),
        out_specs=tuple(VMEM if shape.shape[0] < rows else HBM for shape in shapes),
        scratch_shapes=scratch,
        input_output_aliases=aliases,
        compiler_params=pltpu.CompilerParams(vmem_limit_bytes=16 << 20),
        cost_estimate=pl.CostEstimate(flops=flops, bytes_accessed=count * half * cols * 6, transcendentals=0),
        name=name,
    )(*inputs)


def local(features, weight, bias):
    rows, cols, owned, chans = features.shape
    count = lax.axis_size("tile")
    swap = [(0, 1), (1, 0)]
    own = jnp.transpose(features, (0, 2, 3, 1)).reshape(rows, owned * chans, cols)
    other = lax.ppermute(own, "rot", swap)
    near, far, weight = pick_edges(own, weight)

    def pairs(start):
        return [p for k in range(start, count - 1, 2) for p in ((k, k + 1), (k + 1, k))]

    near_own = lax.ppermute(near, "tile", pairs(0))
    far_own = lax.ppermute(far, "tile", pairs(1))
    filt, column = build_filters(weight, bias.reshape(1, chans), owned)
    split = rows // 2 + 1
    line = (owned * weight.shape[3], cols)

    def block(n):
        return jax.ShapeDtypeStruct((n,) + line, jnp.bfloat16)

    inputs = (filt, column, own, other)
    dma = pltpu.SemaphoreType.DMA
    (done,) = call(first_kernel, "first", (block(split - 1),), inputs, [], {}, split - 1)
    near_own, far_own, done = lax.optimization_barrier((near_own, far_own, done))
    near_other = lax.ppermute(near_own, "rot", swap)
    far_other = lax.ppermute(far_own, "rot", swap)
    more = rows - 1 - split
    out, done = call(second_kernel, "second", (block(rows), block(more)), inputs + (done,), [dma], {}, more)
    (out,) = call(
        last_kernel,
        "last",
        (block(rows),),
        inputs + (near_own, near_other, far_own, far_other, done, out),
        [pltpu.VMEM((2,) + line, jnp.bfloat16), dma, dma((2,))],
        {9: 0},
        2,
    )
    return jnp.transpose(out.reshape(rows, owned, chans, cols), (0, 3, 1, 2))


def solution(mesh):
    spec = P(("groups", "tile"), None, "rot", None)
    return jax.shard_map(
        local,
        mesh=mesh,
        in_specs=(spec, P(), P()),
        out_specs=spec,
        check_vma=False,
    )
```

time: 31.7 us -> 29.5 us (0.931)
  the two profiles are of different devices: /device:TPU:7 before, /device:TPU:19 now
where the time goes in v3:
time: 29.5 us; the launch traced here: 29.4 us
  Pallas kernels  23.4 us (79%)
  starting transfers between devices  4.56 us (15%)
  waiting for transfers between devices  1.19 us (4%)
    pallas_call x3, Pallas kernels, call(): pl.pallas_call(kernel, out_shape=shapes, in_specs=[VMEM] * (len(inputs) -...  20.9 us
    ppermute x1, starting transfers between devices, local(): far_own = lax.ppermute(far, 'tile', pairs(1))  2.01 us
    pallas_call x1, Pallas kernels, pick_edges(): pl.pallas_call(pick_kernel, out_shape=(edge, edge, jax.ShapeDtypeStruct(w...  1.8 us
    ppermute x1, starting transfers between devices, local(): near_own = lax.ppermute(near, 'tile', pairs(0))  1.3 us
    ppermute x1, waiting for transfers between devices, local(): other = lax.ppermute(own, 'rot', swap)  1.18 us
    ppermute x1, starting transfers between devices, local(): other = lax.ppermute(own, 'rot', swap)  0.68 us
    pallas_call x1, Pallas kernels, build_filters(): pl.pallas_call(functools.partial(filters_kernel, owned, orient), out_shap...  0.67 us
  transfers between devices with their start and end apart: 5, of which 1 were waited for; matrix products, arithmetic and copies ran while one was open for 0% of the time, Pallas kernels for 68%

profile of v3, /device:TPU:19, one launch (start us, length us, event | category | flops | bytes accessed | tf_op | source)
XLA Modules:
  0.0 29.4 jit_solution(11874755796183927359)
XLA Ops:
  0.0 0.0 copy-start.1
  0.0 0.0 copy-start
  0.0 0.7 %collective-permute-start = (bf16[16,256,512]{2,1,0:T(8,128)(2,1)}, bf16[16,256,512]{2,1,0:T(8,128)(2,1)S(1)}, u32[]{:S(2)}, u32[]{:S(2)}) collective-permute-start(bf16[16,256,512]{2,1,0:T(8,128)(2,1)} %bitcast.7), channel_id=1, source_target_pairs={{0,1},{1,0},{2,3},{3,2},{4,5},{5,4},{6,7},{7,6},{8,9},{9,8},{10,11... | collective-permute-start | bytes 12582920 | tf_op jit(solution)/shard_map/ppermute | solution.py:173
  0.7 1.8 %pick.1 = (bf16[1,256,512]{2,1,0:T(8,128)(2,1)S(1)}, bf16[1,256,512]{2,1,0:T(8,128)(2,1)S(1)}, bf16[8,9,64,64]{3,2,1,0:T(8,128)(2,1)S(1)}) custom-call(bf16[16,256,512]{2,1,0:T(8,128)(2,1)} %bitcast.8, bf16[8,9,64,64]{3,2,1,0:T(8,128)(2,1)} %weight_hbm.1), custom_call_target="tpu_custom_call" | custom-call | tf_op jit(solution)/shard_map/pick/pallas_call | solution.py:78
  2.5 1.3 %collective-permute-start.1 = (bf16[1,256,512]{2,1,0:T(8,128)(2,1)S(1)}, bf16[1,256,512]{2,1,0:T(8,128)(2,1)S(1)}, u32[]{:S(2)}, u32[]{:S(2)}) collective-permute-start(bf16[1,256,512]{2,1,0:T(8,128)(2,1)S(1)} %get-tuple-element.18), channel_id=1, source_target_pairs={{0,2},{2,0},{4,6},{6,4},{8,10},{10,8},{12,14},{14,12},{1,3},{3,1},... | collective-permute-start | bytes 786440 | tf_op jit(solution)/shard_map/ppermute | solution.py:179
  3.8 2.0 %collective-permute-start.2 = (bf16[1,256,512]{2,1,0:T(8,128)(2,1)S(1)}, bf16[1,256,512]{2,1,0:T(8,128)(2,1)S(1)}, u32[]{:S(2)}, u32[]{:S(2)}) collective-permute-start(bf16[1,256,512]{2,1,0:T(8,128)(2,1)S(1)} %get-tuple-element.19), channel_id=1, source_target_pairs={{2,4},{4,2},{6,8},{8,6},{10,12},{12,10},{3,5},{5,3},{7,9},{9,7},{1... | collective-permute-start | bytes 786440 | tf_op jit(solution)/shard_map/ppermute | solution.py:180
  5.8 0.0 copy-done.1
  5.8 0.7 %filters.1 = (bf16[9,256,512]{2,1,0:T(8,128)(2,1)S(1)}, f32[256,128]{1,0:T(8,128)S(1)}) custom-call(bf16[8,9,64,64]{3,2,1,0:T(8,128)(2,1)S(1)} %get-tuple-element.15.weight_ref, f32[1,64]{1,0:T(1,128)S(1)} %bitcast.12), custom_call_target="tpu_custom_call" | custom-call | tf_op jit(solution)/shard_map/filters/pallas_call | solution.py:48
  6.5 1.2 %collective-permute-done.other = bf16[16,256,512]{2,1,0:T(8,128)(2,1)S(1)} collective-permute-done((bf16[16,256,512]{2,1,0:T(8,128)(2,1)}, bf16[16,256,512]{2,1,0:T(8,128)(2,1)S(1)}, u32[]{:S(2)}, u32[]{:S(2)}) %collective-permute-start) | collective-permute-done | bytes 4194336 | tf_op jit(solution)/shard_map/ppermute | solution.py:173
  7.7 0.0 copy-done
  7.7 9.9 %first.1.done = bf16[8,256,512]{2,1,0:T(8,128)(2,1)S(1)} custom-call(bf16[9,256,512]{2,1,0:T(8,128)(2,1)S(1)} %get-tuple-element.16.filt, f32[256,128]{1,0:T(8,128)S(1)} %get-tuple-element.17.column, bf16[16,256,512]{2,1,0:T(8,128)(2,1)S(1)} %bitcast.9, bf16[16,256,512]{2,1,0:T(8,128)(2,1)S(1)} %collective-permute-done.other), custom_call_target="tpu_custom_call" | custom-call | flops 9663676416 | bytes 6291456 | tf_op jit(solution)/shard_map/first/pallas_call | solution.py:155
  17.6 0.0 collective-permute-done.1.near_own
  17.6 0.0 collective-permute-done.2.far_own
  17.6 0.4 %collective-permute-start.3 = (bf16[1,256,512]{2,1,0:T(8,128)(2,1)S(1)}, bf16[1,256,512]{2,1,0:T(8,128)(2,1)S(1)}, u32[]{:S(2)}, u32[]{:S(2)}) collective-permute-start(bf16[1,256,512]{2,1,0:T(8,128)(2,1)S(1)} %collective-permute-done.1.near_own), channel_id=1, source_target_pairs={{0,1},{1,0},{2,3},{3,2},{4,5},{5,4},{6,7},{7,6},{8,9},{9,8},{10,11... | collective-permute-start | bytes 786440 | tf_op jit(solution)/shard_map/ppermute | solution.py:192
  18.0 0.1 collective-permute-start.4
  18.2 7.7 %second.1 = (bf16[16,256,512]{2,1,0:T(8,128)(2,1)}, bf16[6,256,512]{2,1,0:T(8,128)(2,1)S(1)}) custom-call(bf16[9,256,512]{2,1,0:T(8,128)(2,1)S(1)} %get-tuple-element.16.filt, f32[256,128]{1,0:T(8,128)S(1)} %get-tuple-element.17.column, bf16[16,256,512]{2,1,0:T(8,128)(2,1)S(1)} %bitcast.10, bf16[16,256,512]{2,1,0:T(8,128)(2,1)S(1)} %collective-permute-done.other, ...), custom_call_target="tpu_custom_call" | custom-call | flops 7247757312 | bytes 4718592 | tf_op jit(solution)/shard_map/second/pallas_call | solution.py:155
  25.9 0.0 collective-permute-done.3.near_other
  25.9 0.0 collective-permute-done.4.far_other
  25.9 3.3 %last.1 = bf16[16,256,512]{2,1,0:T(8,128)(2,1)} custom-call(bf16[9,256,512]{2,1,0:T(8,128)(2,1)S(1)} %get-tuple-element.16.filt, f32[256,128]{1,0:T(8,128)S(1)} %get-tuple-element.17.column, bf16[16,256,512]{2,1,0:T(8,128)(2,1)S(1)} %bitcast.11, bf16[16,256,512]{2,1,0:T(8,128)(2,1)S(1)} %collective-permute-done.other, ...), custom_call_target="tpu_custom_call", output_to_operand_aliasing={{}: (9, {})} | custom-call | flops 2415919104 | bytes 1572864 | tf_op jit(solution)/shard_map/last/pallas_call | solution.py:155
Async XLA Ops:
  0.0 5.8 %copy-start.1 = (f32[64]{0:T(128)S(1)}, f32[64]{0:T(128)}, u32[]{:S(2)}) copy-start(f32[64]{0:T(128)} %param.5) | copy-start | bytes 772
  0.0 7.7 %copy-start = (bf16[16,512,4,64]{1,3,2,0:T(8,128)(2,1)S(1)}, bf16[16,512,4,64]{1,3,2,0:T(8,128)(2,1)}, u32[]{:S(2)}) copy-start(bf16[16,512,4,64]{1,3,2,0:T(8,128)(2,1)} %param.3) | copy-start | bytes 12582916
  0.0 7.7 %collective-permute-start = (bf16[16,256,512]{2,1,0:T(8,128)(2,1)}, bf16[16,256,512]{2,1,0:T(8,128)(2,1)S(1)}, u32[]{:S(2)}, u32[]{:S(2)}) collective-permute-start(bf16[16,256,512]{2,1,0:T(8,128)(2,1)} %bitcast.7), channel_id=1, source_target_pairs={{0,1},{1,0},{2,3},{3,2},{4,5},{5,4},{6,7},{7,6},{8,9},{9,8},{10,11... | collective-permute-start | bytes 12582920 | tf_op jit(solution)/shard_map/ppermute | solution.py:173
  2.5 15.1 %collective-permute-start.1 = (bf16[1,256,512]{2,1,0:T(8,128)(2,1)S(1)}, bf16[1,256,512]{2,1,0:T(8,128)(2,1)S(1)}, u32[]{:S(2)}, u32[]{:S(2)}) collective-permute-start(bf16[1,256,512]{2,1,0:T(8,128)(2,1)S(1)} %get-tuple-element.18), channel_id=1, source_target_pairs={{0,2},{2,0},{4,6},{6,4},{8,10},{10,8},{12,14},{14,12},{1,3},{3,1},... | collective-permute-start | bytes 786440 | tf_op jit(solution)/shard_map/ppermute | solution.py:179
  3.8 13.8 %collective-permute-start.2 = (bf16[1,256,512]{2,1,0:T(8,128)(2,1)S(1)}, bf16[1,256,512]{2,1,0:T(8,128)(2,1)S(1)}, u32[]{:S(2)}, u32[]{:S(2)}) collective-permute-start(bf16[1,256,512]{2,1,0:T(8,128)(2,1)S(1)} %get-tuple-element.19), channel_id=1, source_target_pairs={{2,4},{4,2},{6,8},{8,6},{10,12},{12,10},{3,5},{5,3},{7,9},{9,7},{1... | collective-permute-start | bytes 786440 | tf_op jit(solution)/shard_map/ppermute | solution.py:180
  17.6 8.3 %collective-permute-start.3 = (bf16[1,256,512]{2,1,0:T(8,128)(2,1)S(1)}, bf16[1,256,512]{2,1,0:T(8,128)(2,1)S(1)}, u32[]{:S(2)}, u32[]{:S(2)}) collective-permute-start(bf16[1,256,512]{2,1,0:T(8,128)(2,1)S(1)} %collective-permute-done.1.near_own), channel_id=1, source_target_pairs={{0,1},{1,0},{2,3},{3,2},{4,5},{5,4},{6,7},{7,6},{8,9},{9,8},{10,11... | collective-permute-start | bytes 786440 | tf_op jit(solution)/shard_map/ppermute | solution.py:192
  18.0 7.8 %collective-permute-start.4 = (bf16[1,256,512]{2,1,0:T(8,128)(2,1)S(1)}, bf16[1,256,512]{2,1,0:T(8,128)(2,1)S(1)}, u32[]{:S(2)}, u32[]{:S(2)}) collective-permute-start(bf16[1,256,512]{2,1,0:T(8,128)(2,1)S(1)} %collective-permute-done.2.far_own), channel_id=1, source_target_pairs={{0,1},{1,0},{2,3},{3,2},{4,5},{5,4},{6,7},{7,6},{8,9},{9,8},{10,11... | collective-permute-start | bytes 786440 | tf_op jit(solution)/shard_map/ppermute | solution.py:193

commit v4 on v3

--- a/solution.py
+++ b/solution.py
@@ -93,12 +93,12 @@
     return jnp.where((place >= 0) & (place < cols), turned, jnp.zeros_like(turned))
 
 
-def row_sums(filt, lines, column):
+def row_sums(filt, lines, column, order=(0, 1, 2)):
     half = filt.shape[2] // 2
     acc = None
     for b in (1, 0, 2):
-        for a, line in enumerate(lines):
-            for which, part in enumerate(line):
+        for a in order:
+            for which, part in enumerate(lines[a]):
                 term = jnp.dot(
                     filt[3 * a + b, :, which * half : (which + 1) * half],
                     part if b == 1 else shifted(part, b - 1),
@@ -130,18 +130,19 @@
 
 
 def last_kernel(
-    filt, column, own, other, near_own, near_other, far_own, far_other, done, partial, out_hbm, out, sem, out_sem
+    filt, column, own, other, halo, halo_other, done, partial, out_hbm, out, sem, out_sem
 ):
     rows = own.shape[0]
     copies = [send(done, out_hbm, rows - 1 - done.shape[0], sem)]
     copies[0].start()
     even = lax.rem(lax.axis_index("tile"), 2) == 0
-    pairs = ((near_own[0], far_own[0]), (near_other[0], far_other[0]))
+    pairs = ((halo[0], halo[1]), (halo_other[0], halo_other[1]))
     above = [jnp.where(even, far, near) for near, far in pairs]
     below = [jnp.where(even, near, far) for near, far in pairs]
     for k, y in enumerate((0, rows - 1)):
         body = [(own[j], other[j]) for j in ((0, 1), (rows - 2, rows - 1))[k]]
-        out[k] = row_sums(filt, [above] + body if k == 0 else body + [below], column[...])
+        lines = [above] + body if k == 0 else body + [below]
+        out[k] = row_sums(filt, lines, column[...], (1, 2, 0) if k == 0 else (0, 1, 2))
         copies.append(pltpu.make_async_copy(out.at[k], out_hbm.at[y], out_sem.at[k]))
         copies[-1].start()
     for copy in copies:
@@ -189,17 +190,17 @@
     dma = pltpu.SemaphoreType.DMA
     (done,) = call(first_kernel, "first", (block(split - 1),), inputs, [], {}, split - 1)
     near_own, far_own, done = lax.optimization_barrier((near_own, far_own, done))
-    near_other = lax.ppermute(near_own, "rot", swap)
-    far_other = lax.ppermute(far_own, "rot", swap)
+    halo = jnp.concatenate([near_own, far_own], 0)
+    halo_other = lax.ppermute(halo, "rot", swap)
     more = rows - 1 - split
     out, done = call(second_kernel, "second", (block(rows), block(more)), inputs + (done,), [dma], {}, more)
     (out,) = call(
         last_kernel,
         "last",
         (block(rows),),
-        inputs + (near_own, near_other, far_own, far_other, done, out),
+        inputs + (halo, halo_other, done, out),
         [pltpu.VMEM((2,) + line, jnp.bfloat16), dma, dma((2,))],
-        {9: 0},
+        {7: 0},
         2,
     )
     return jnp.transpose(out.reshape(rows, owned, chans, cols), (0, 3, 1, 2))

time: 29.5 us -> 29.4 us (level)
  transfers between devices with their start and end apart: 5 -> 4, of which waited for: 1 -> 1; matrix products, arithmetic and copies ran while one was open for 0% -> 0% of each run, Pallas kernels for 68% -> 68%
where the time goes in v4:
time: 29.4 us; the launch traced here: 29.3 us
  Pallas kernels  23.4 us (80%)
  starting transfers between devices  4.43 us (15%)
  waiting for transfers between devices  1.19 us (4%)
    pallas_call x3, Pallas kernels, call(): pl.pallas_call(kernel, out_shape=shapes, in_specs=[VMEM] * (len(inputs) -...  20.9 us
    ppermute x1, starting transfers between devices, local(): far_own = lax.ppermute(far, 'tile', pairs(1))  2.01 us
    pallas_call x1, Pallas kernels, pick_edges(): pl.pallas_call(pick_kernel, out_shape=(edge, edge, jax.ShapeDtypeStruct(w...  1.8 us
    ppermute x1, starting transfers between devices, local(): near_own = lax.ppermute(near, 'tile', pairs(0))  1.3 us
    ppermute x1, waiting for transfers between devices, local(): other = lax.ppermute(own, 'rot', swap)  1.18 us
    ppermute x1, starting transfers between devices, local(): other = lax.ppermute(own, 'rot', swap)  0.68 us
    pallas_call x1, Pallas kernels, build_filters(): pl.pallas_call(functools.partial(filters_kernel, owned, orient), out_shap...  0.67 us
  transfers between devices with their start and end apart: 4, of which 1 were waited for; matrix products, arithmetic and copies ran while one was open for 0% of the time, Pallas kernels for 68%

profile of v4, /device:TPU:19, one launch (start us, length us, event | category | flops | bytes accessed | tf_op | source)
XLA Modules:
  0.0 29.3 jit_solution(15388043749354484863)
XLA Ops:
  0.0 0.0 copy-start.1
  0.0 0.0 copy-start
  0.0 0.7 %collective-permute-start = (bf16[16,256,512]{2,1,0:T(8,128)(2,1)}, bf16[16,256,512]{2,1,0:T(8,128)(2,1)S(1)}, u32[]{:S(2)}, u32[]{:S(2)}) collective-permute-start(bf16[16,256,512]{2,1,0:T(8,128)(2,1)} %bitcast.7), channel_id=1, source_target_pairs={{0,1},{1,0},{2,3},{3,2},{4,5},{5,4},{6,7},{7,6},{8,9},{9,8},{10,11... | collective-permute-start | bytes 12582920 | tf_op jit(solution)/shard_map/ppermute | solution.py:174
  0.7 1.8 %pick.1 = (bf16[1,256,512]{2,1,0:T(8,128)(2,1)S(1)}, bf16[1,256,512]{2,1,0:T(8,128)(2,1)S(1)}, bf16[8,9,64,64]{3,2,1,0:T(8,128)(2,1)S(1)}) custom-call(bf16[16,256,512]{2,1,0:T(8,128)(2,1)} %bitcast.8, bf16[8,9,64,64]{3,2,1,0:T(8,128)(2,1)} %weight_hbm.1), custom_call_target="tpu_custom_call" | custom-call | tf_op jit(solution)/shard_map/pick/pallas_call | solution.py:78
  2.5 1.3 %collective-permute-start.1 = (bf16[1,256,512]{2,1,0:T(8,128)(2,1)S(1)}, bf16[1,256,512]{2,1,0:T(8,128)(2,1)S(1)}, u32[]{:S(2)}, u32[]{:S(2)}) collective-permute-start(bf16[1,256,512]{2,1,0:T(8,128)(2,1)S(1)} %get-tuple-element.18), channel_id=1, source_target_pairs={{0,2},{2,0},{4,6},{6,4},{8,10},{10,8},{12,14},{14,12},{1,3},{3,1},... | collective-permute-start | bytes 786440 | tf_op jit(solution)/shard_map/ppermute | solution.py:180
  3.8 2.0 %collective-permute-start.2 = (bf16[1,256,512]{2,1,0:T(8,128)(2,1)S(1)}, bf16[1,256,512]{2,1,0:T(8,128)(2,1)S(1)}, u32[]{:S(2)}, u32[]{:S(2)}) collective-permute-start(bf16[1,256,512]{2,1,0:T(8,128)(2,1)S(1)} %get-tuple-element.19), channel_id=1, source_target_pairs={{2,4},{4,2},{6,8},{8,6},{10,12},{12,10},{3,5},{5,3},{7,9},{9,7},{1... | collective-permute-start | bytes 786440 | tf_op jit(solution)/shard_map/ppermute | solution.py:181
  5.8 0.0 copy-done.1
  5.8 0.7 %filters.1 = (bf16[9,256,512]{2,1,0:T(8,128)(2,1)S(1)}, f32[256,128]{1,0:T(8,128)S(1)}) custom-call(bf16[8,9,64,64]{3,2,1,0:T(8,128)(2,1)S(1)} %get-tuple-element.15.weight_ref, f32[1,64]{1,0:T(1,128)S(1)} %bitcast.12), custom_call_target="tpu_custom_call" | custom-call | tf_op jit(solution)/shard_map/filters/pallas_call | solution.py:48
  6.5 1.2 %collective-permute-done.other = bf16[16,256,512]{2,1,0:T(8,128)(2,1)S(1)} collective-permute-done((bf16[16,256,512]{2,1,0:T(8,128)(2,1)}, bf16[16,256,512]{2,1,0:T(8,128)(2,1)S(1)}, u32[]{:S(2)}, u32[]{:S(2)}) %collective-permute-start) | collective-permute-done | bytes 4194336 | tf_op jit(solution)/shard_map/ppermute | solution.py:174
  7.7 0.0 copy-done
  7.7 9.9 %first.1.done = bf16[8,256,512]{2,1,0:T(8,128)(2,1)S(1)} custom-call(bf16[9,256,512]{2,1,0:T(8,128)(2,1)S(1)} %get-tuple-element.16.filt, f32[256,128]{1,0:T(8,128)S(1)} %get-tuple-element.17.column, bf16[16,256,512]{2,1,0:T(8,128)(2,1)S(1)} %bitcast.9, bf16[16,256,512]{2,1,0:T(8,128)(2,1)S(1)} %collective-permute-done.other), custom_call_target="tpu_custom_call" | custom-call | flops 9663676416 | bytes 6291456 | tf_op jit(solution)/shard_map/first/pallas_call | solution.py:156
  17.6 0.0 collective-permute-done.1
  17.6 0.0 collective-permute-done.2
  17.6 0.4 %collective-permute-start.3 = (bf16[2,256,512]{2,1,0:T(8,128)(2,1)S(1)}, bf16[2,256,512]{2,1,0:T(8,128)(2,1)S(1)}, u32[]{:S(2)}, u32[]{:S(2)}) collective-permute-start(bf16[2,256,512]{2,1,0:T(8,128)(2,1)S(1)} %constant_dynamic-update-slice_fusion.halo), channel_id=1, source_target_pairs={{0,1},{1,0},{2,3},{3,2},{4,5},{5,4},{6,7},{7,6},{8,9},{9,8},{10,11... | collective-permute-start | bytes 1572872 | tf_op jit(solution)/shard_map/ppermute | solution.py:194
  18.1 7.7 %second.1 = (bf16[16,256,512]{2,1,0:T(8,128)(2,1)}, bf16[6,256,512]{2,1,0:T(8,128)(2,1)S(1)}) custom-call(bf16[9,256,512]{2,1,0:T(8,128)(2,1)S(1)} %get-tuple-element.16.filt, f32[256,128]{1,0:T(8,128)S(1)} %get-tuple-element.17.column, bf16[16,256,512]{2,1,0:T(8,128)(2,1)S(1)} %bitcast.10, bf16[16,256,512]{2,1,0:T(8,128)(2,1)S(1)} %collective-permute-done.other, ...), custom_call_target="tpu_custom_call" | custom-call | flops 7247757312 | bytes 4718592 | tf_op jit(solution)/shard_map/second/pallas_call | solution.py:156
  25.8 0.0 collective-permute-done.3.halo_other
  25.8 3.3 %last.1 = bf16[16,256,512]{2,1,0:T(8,128)(2,1)} custom-call(bf16[9,256,512]{2,1,0:T(8,128)(2,1)S(1)} %get-tuple-element.16.filt, f32[256,128]{1,0:T(8,128)S(1)} %get-tuple-element.17.column, bf16[16,256,512]{2,1,0:T(8,128)(2,1)S(1)} %bitcast.11, bf16[16,256,512]{2,1,0:T(8,128)(2,1)S(1)} %collective-permute-done.other, ...), custom_call_target="tpu_custom_call", output_to_operand_aliasing={{}: (7, {})} | custom-call | flops 2415919104 | bytes 1572864 | tf_op jit(solution)/shard_map/last/pallas_call | solution.py:156
  (2 shorter events, 0.0 us)
Async XLA Ops:
  0.0 5.8 %copy-start.1 = (f32[64]{0:T(128)S(1)}, f32[64]{0:T(128)}, u32[]{:S(2)}) copy-start(f32[64]{0:T(128)} %param.5) | copy-start | bytes 772
  0.0 7.7 %copy-start = (bf16[16,512,4,64]{1,3,2,0:T(8,128)(2,1)S(1)}, bf16[16,512,4,64]{1,3,2,0:T(8,128)(2,1)}, u32[]{:S(2)}) copy-start(bf16[16,512,4,64]{1,3,2,0:T(8,128)(2,1)} %param.3) | copy-start | bytes 12582916
  0.0 7.7 %collective-permute-start = (bf16[16,256,512]{2,1,0:T(8,128)(2,1)}, bf16[16,256,512]{2,1,0:T(8,128)(2,1)S(1)}, u32[]{:S(2)}, u32[]{:S(2)}) collective-permute-start(bf16[16,256,512]{2,1,0:T(8,128)(2,1)} %bitcast.7), channel_id=1, source_target_pairs={{0,1},{1,0},{2,3},{3,2},{4,5},{5,4},{6,7},{7,6},{8,9},{9,8},{10,11... | collective-permute-start | bytes 12582920 | tf_op jit(solution)/shard_map/ppermute | solution.py:174
  2.5 15.1 %collective-permute-start.1 = (bf16[1,256,512]{2,1,0:T(8,128)(2,1)S(1)}, bf16[1,256,512]{2,1,0:T(8,128)(2,1)S(1)}, u32[]{:S(2)}, u32[]{:S(2)}) collective-permute-start(bf16[1,256,512]{2,1,0:T(8,128)(2,1)S(1)} %get-tuple-element.18), channel_id=1, source_target_pairs={{0,2},{2,0},{4,6},{6,4},{8,10},{10,8},{12,14},{14,12},{1,3},{3,1},... | collective-permute-start | bytes 786440 | tf_op jit(solution)/shard_map/ppermute | solution.py:180
  3.8 13.8 %collective-permute-start.2 = (bf16[1,256,512]{2,1,0:T(8,128)(2,1)S(1)}, bf16[1,256,512]{2,1,0:T(8,128)(2,1)S(1)}, u32[]{:S(2)}, u32[]{:S(2)}) collective-permute-start(bf16[1,256,512]{2,1,0:T(8,128)(2,1)S(1)} %get-tuple-element.19), channel_id=1, source_target_pairs={{2,4},{4,2},{6,8},{8,6},{10,12},{12,10},{3,5},{5,3},{7,9},{9,7},{1... | collective-permute-start | bytes 786440 | tf_op jit(solution)/shard_map/ppermute | solution.py:181
  17.6 8.1 %collective-permute-start.3 = (bf16[2,256,512]{2,1,0:T(8,128)(2,1)S(1)}, bf16[2,256,512]{2,1,0:T(8,128)(2,1)S(1)}, u32[]{:S(2)}, u32[]{:S(2)}) collective-permute-start(bf16[2,256,512]{2,1,0:T(8,128)(2,1)S(1)} %constant_dynamic-update-slice_fusion.halo), channel_id=1, source_target_pairs={{0,1},{1,0},{2,3},{3,2},{4,5},{5,4},{6,7},{7,6},{8,9},{9,8},{10,11... | collective-permute-start | bytes 1572872 | tf_op jit(solution)/shard_map/ppermute | solution.py:194
